TPU v7x, 32 devices: a whole 2x2x4 slice. The times are simulated.
32 devices in a mesh: groups: 2 (over y), sec: 4 (over x, core), tile: 4 (over z).
Axes of the slice: x: 2, y: 2, z: 4, core: 2. Of those that a mesh axis runs over, the one named last changes fastest.
Arguments:
- raw_image: float32 [8, 128, 256], P(('groups', 'sec'), 'tile'), parts along dimension 0, may hold values from -6 to 6
- pairing: int32 [8], P(('groups', 'sec')), parts along dimension 0, may hold values from 0 to 3, as said below
- valid_mask: int32 [8, 4, 8], P(('groups', 'sec'), 'tile'), parts along dimension 0, may hold values 0 or 1
- first_kernel: float32 [32, 1, 3, 3], replicated, may hold values from -2 to 2
- later_kernels: float32 [2, 32, 32, 3, 3], replicated, may hold values from -0.375 to 0.375
- biases: float32 [3, 32], replicated, may hold values from -0.6 to 0.6
Outputs:
- correlation: float32 [8, 4, 8, 289], P(('groups', 'sec'), 'tile'), parts along dimension 0
There are 2 independent parts, one for each index of `groups`. A program takes and returns all parts, laid end to end along the dimension named above; an argument that names none is the same for every part. Nothing has to cross between parts.
Inputs may be any that keep to these rules, and one draw needn't show every extreme that they name: pairing[pairing[s]] = s and pairing[s] is s - 1, s or s + 1; all pairs of one list begin at sections of the same parity, and a section without a partner is paired with itself.
All inputs are finite; a program needn't handle non-finite values. No bound on the sum of `valid_mask` on one device may be relied on, other than what follows from the above.
Results may differ from a plain program's by a relative error of at most 0.0001.
Values sent between devices are 32-bit elements; how exact they have to be, the bound alone decides.
No kernel may reach another device: no remote copies, remote signals or barrier semaphores. Data moves between devices by JAX's collectives and lax.ppermute only.
A program may use at most 128 MiB of HBM per device.

v0:
```python
import jax
import jax.numpy as jnp
from jax import lax
from jax.sharding import PartitionSpec as P

LAYERS = 3
BLK = 32
RADIUS = 8


def with_halo(array, sides, width):
    for axis, dim in sides:
        devices, length = (lax.axis_size(axis), array.shape[dim])
        up = [(i, (i + 1) % devices) for i in range(devices - 1)]
        down = [(j, i) for i, j in up]
        last = lax.slice_in_dim(array, length - width, length, axis=dim)
        first = lax.slice_in_dim(array, 0, width, axis=dim)
        before = lax.ppermute(last, axis, up)
        after = lax.ppermute(first, axis, down)
        array = jnp.concatenate([before, array, after], axis=dim)
    return array


def from_behind(value, axis, steps):
    count = lax.axis_size(axis)
    first, last = (max(0, -steps), min(count, count - steps))
    return lax.ppermute(value, axis, [(source, source + steps) for source in range(first, last)])


def apply_layer(current, kernel, bias, final_layer):
    result = lax.conv_general_dilated(
        current[None],
        kernel,
        (1, 1),
        ((0, 0), (1, 1)),
        dimension_numbers=("NCHW", "OIHW", "NCHW"),
        precision=lax.Precision.HIGHEST,
    )[0]
    result = result + bias[:, None, None]
    if final_layer:
        return result
    return jnp.tanh(result)


def correlate(own_feats, padded):
    channels, strip_rows, width = own_feats.shape
    block_rows = strip_rows // BLK
    block_cols = width // BLK
    span = BLK + 2 * RADIUS
    widened = jnp.pad(padded, ((0, 0), (0, 0), (RADIUS, BLK - RADIUS)))
    leading = widened[:, :, :width].reshape(channels, strip_rows + 2 * RADIUS, block_cols, BLK)
    second = widened[:, :, BLK : BLK + width].reshape(
        channels, strip_rows + 2 * RADIUS, block_cols, BLK
    )[..., : 2 * RADIUS]
    windows = jnp.concatenate([leading, second], axis=-1).reshape(
        channels, strip_rows + 2 * RADIUS, block_cols * span
    )
    blocks = own_feats.reshape(channels, block_rows, BLK, block_cols, BLK)
    column = jnp.arange(BLK, dtype=jnp.int32)[:, None, None]
    target = jnp.arange(span, dtype=jnp.int32)[None, :, None]
    moved = jnp.arange(2 * RADIUS + 1, dtype=jnp.int32)[None, None, :]
    picker = (target == column + moved).astype(jnp.float32)

    def one_shift(offset):
        strip_band = lax.dynamic_slice_in_dim(windows, offset, strip_rows, 1)
        strip_band = strip_band.reshape(channels, block_rows, BLK, block_cols, span)
        products = jnp.einsum(
            "cnybx,cnybz->nbxz", blocks, strip_band, precision=lax.Precision.HIGHEST
        )
        return jnp.einsum("nbxz,xzd->nbd", products, picker, precision=lax.Precision.HIGHEST)

    shifted = lax.map(one_shift, jnp.arange(2 * RADIUS + 1, dtype=jnp.int32))
    shifted = jnp.transpose(shifted, (1, 2, 0, 3)).reshape(
        block_rows, block_cols, (2 * RADIUS + 1) ** 2
    )
    return shifted / jnp.sqrt(jnp.float32(BLK * BLK * channels))


def choose_partner(pairing, section, own_value, from_below, from_above):
    direction = pairing[0] - section
    return jnp.where(direction < 0, from_below, jnp.where(direction > 0, from_above, own_value))


def body(raw_image, pairing, valid_mask, first_kernel, later_kernels, biases):
    section = lax.axis_index("sec")
    kernels = [first_kernel] + [later_kernels[layer] for layer in range(LAYERS - 1)]
    current = raw_image
    for layer in range(LAYERS):
        current = with_halo(current, (("tile", 1),), 1)
        current = apply_layer(current, kernels[layer], biases[layer], layer == LAYERS - 1)
    from_below = from_behind(current, "sec", 1)
    from_above = from_behind(current, "sec", -1)
    partner = choose_partner(pairing, section, current, from_below, from_above)
    padded = with_halo(partner, (("tile", 1),), RADIUS)
    weights = valid_mask[0].astype(jnp.float32)
    result = correlate(current, padded) * weights[:, :, None]
    return result[None]


def solution(mesh):
    placed = (
        P(("groups", "sec"), "tile", None),
        P(("groups", "sec")),
        P(("groups", "sec"), "tile", None),
        P(),
        P(),
        P(),
    )
    return jax.shard_map(
        body,
        mesh=mesh,
        in_specs=placed,
        out_specs=P(("groups", "sec"), "tile", None, None),
        check_vma=False,
    )
```

profile of v0, /device:TPU:1, one launch (start us, length us, event | category | flops | bytes accessed | tf_op | source)
XLA Modules:
  0.0 520.6 jit_solution(5236094361581456541)
XLA Ops:
  10.7 16.4 %broadcast_select_fusion.2 = f32[32,8,33,32]{3,1,2,0:T(8,128)} fusion(pred[8,33]{0,1:T(8,128)(4,1)} %constant.40, f32[32,1,3,3]{0,1,3,2:T(1,128)S(1)} %copy-done, f32[1,34,1,8,35]{3,0,4,2,1:T(1,128)S(1)} %copy.36), kind=kOutput, calls=%fused_computation.35 | convolution fusion | flops 29466624 | bytes 1120840 | tf_op jit(solution)/shard_map/conv_general_dilated | solution.py:31
  27.0 6.2 %copy.37 = f32[32,8,33,32]{2,1,3,0:T(8,128)} copy(f32[32,8,33,32]{3,1,2,0:T(8,128)} %broadcast_select_fusion.2) | data formatting | bytes 2162688 | tf_op jit(solution)/shard_map/conv_general_dilated | solution.py:31
  55.7 38.4 %broadcast_select_fusion.1 = f32[32,8,33,32]{3,1,2,0:T(8,128)} fusion(pred[8,33]{0,1:T(8,128)(4,1)S(1)} %copy-done.5, f32[32,34,1,7,2]{0,3,4,1,2:T(8,128)S(1)} %slice.74, f32[32,34,1,8,33]{0,3,4,1,2:T(8,128)} %copy.39, f32[2,32,32,3,3]{2,1,4,3,0:T(8,128)S(1)} %copy-done.3), kind=kOutput, calls=%fused_computation.34 | convolution fusion | flops 935465472 | bytes 2661376 | tf_op jit(solution)/shard_map/conv_general_dilated | solution.py:31
  122.6 38.4 %broadcast_select_fusion = f32[32,8,33,32]{3,1,2,0:T(8,128)} fusion(pred[8,33]{0,1:T(8,128)(4,1)S(1)} %copy-done.5, f32[32,34,1,7,2]{0,3,4,1,2:T(8,128)S(1)} %slice.78, f32[32,34,1,8,33]{0,3,4,1,2:T(8,128)} %copy.42, f32[2,32,32,3,3]{2,1,4,3,0:T(8,128)S(1)} %copy-done.3), kind=kOutput, calls=%fused_computation.33 | convolution fusion | flops 935465472 | bytes 2661376 | tf_op jit(solution)/shard_map/conv_general_dilated | solution.py:31
  171.8 8.0 %collective-permute-start.6 = (f32[32,32,256]{2,0,1:T(8,128)}, f32[32,32,256]{2,0,1:T(8,128)}, u32[]{:S(2)}, u32[]{:S(2)}) collective-permute-start(f32[32,32,256]{2,0,1:T(8,128)} %bitcast_add_fusion), channel_id=1, source_target_pairs={{0,4},{4,8},{8,12},{1,5},{5,9},{9,13},{2,6},{6,10},{10,14},{3,7},{... | collective-permute-start | bytes 3145736 | tf_op jit(solution)/shard_map/ppermute | solution.py:27
  217.5 8.9 %pad_maximum_fusion = f32[32,48,8,48]{3,2,1,0:T(8,128)} fusion(f32[32,48,8,16]{3,2,1,0:T(8,128)} %bitcast.114, f32[32,48,8,32]{3,2,1,0:T(8,128)} %reshape.96), kind=kLoop, calls=%fused_computation.12 | loop fusion | flops 589824 | bytes 4718592 | tf_op jit(solution)/shard_map/concatenate | solution.py:55
  232.3 287.0 %while.11 = (s32[]{:T(128)}, f32[17,1,8,17]{3,2,1,0:T(8,128)S(1)}, s32[17]{0:T(128)S(1)}, f32[32,48,384]{2,1,0:T(8,128)}, f32[32,1,32,8,32]{2,4,0,3,1:T(8,128)},...) while((s32[]{:T(128)}, f32[17,1,8,17]{3,2,1,0:T(8,128)S(1)}, s32[17]{0:T(128)S(1)}, ...), condition=%wide.region_1.2_spmd.clone, body=%wide.region_0.1_spmd.clone.sunk | while | flops 153553920 | bytes 9113747 | solution.py:72
  239.5 9.1 %fusion.64 = f32[8,32,48]{2,1,0:T(8,128)S(1)} fusion(f32[32,1,32,8,32]{2,4,0,3,1:T(8,128)} %get-tuple-element.137, f32[32,32,8,48]{3,2,1,0:T(8,128)} %reshape.141), kind=kOutput, calls=%fused_computation.4.clone.1 | convolution fusion | flops 150994944 | bytes 2670592 | tf_op jit(solution)/shard_map/while/body/eval_jaxpr/cnybx,cnybz->nbxz/dot_general | solution.py:67
  256.4 9.1 %fusion.64 = f32[8,32,48]{2,1,0:T(8,128)S(1)} fusion(f32[32,1,32,8,32]{2,4,0,3,1:T(8,128)} %get-tuple-element.137, f32[32,32,8,48]{3,2,1,0:T(8,128)} %reshape.141), kind=kOutput, calls=%fused_computation.4.clone.1 | convolution fusion | flops 150994944 | bytes 2670592 | tf_op jit(solution)/shard_map/while/body/eval_jaxpr/cnybx,cnybz->nbxz/dot_general | solution.py:67
  273.3 9.1 %fusion.64 = f32[8,32,48]{2,1,0:T(8,128)S(1)} fusion(f32[32,1,32,8,32]{2,4,0,3,1:T(8,128)} %get-tuple-element.137, f32[32,32,8,48]{3,2,1,0:T(8,128)} %reshape.141), kind=kOutput, calls=%fused_computation.4.clone.1 | convolution fusion | flops 150994944 | bytes 2670592 | tf_op jit(solution)/shard_map/while/body/eval_jaxpr/cnybx,cnybz->nbxz/dot_general | solution.py:67
  290.2 9.1 %fusion.64 = f32[8,32,48]{2,1,0:T(8,128)S(1)} fusion(f32[32,1,32,8,32]{2,4,0,3,1:T(8,128)} %get-tuple-element.137, f32[32,32,8,48]{3,2,1,0:T(8,128)} %reshape.141), kind=kOutput, calls=%fused_computation.4.clone.1 | convolution fusion | flops 150994944 | bytes 2670592 | tf_op jit(solution)/shard_map/while/body/eval_jaxpr/cnybx,cnybz->nbxz/dot_general | solution.py:67
  307.1 9.1 %fusion.64 = f32[8,32,48]{2,1,0:T(8,128)S(1)} fusion(f32[32,1,32,8,32]{2,4,0,3,1:T(8,128)} %get-tuple-element.137, f32[32,32,8,48]{3,2,1,0:T(8,128)} %reshape.141), kind=kOutput, calls=%fused_computation.4.clone.1 | convolution fusion | flops 150994944 | bytes 2670592 | tf_op jit(solution)/shard_map/while/body/eval_jaxpr/cnybx,cnybz->nbxz/dot_general | solution.py:67
  324.0 9.1 %fusion.64 = f32[8,32,48]{2,1,0:T(8,128)S(1)} fusion(f32[32,1,32,8,32]{2,4,0,3,1:T(8,128)} %get-tuple-element.137, f32[32,32,8,48]{3,2,1,0:T(8,128)} %reshape.141), kind=kOutput, calls=%fused_computation.4.clone.1 | convolution fusion | flops 150994944 | bytes 2670592 | tf_op jit(solution)/shard_map/while/body/eval_jaxpr/cnybx,cnybz->nbxz/dot_general | solution.py:67
  340.9 9.1 %fusion.64 = f32[8,32,48]{2,1,0:T(8,128)S(1)} fusion(f32[32,1,32,8,32]{2,4,0,3,1:T(8,128)} %get-tuple-element.137, f32[32,32,8,48]{3,2,1,0:T(8,128)} %reshape.141), kind=kOutput, calls=%fused_computation.4.clone.1 | convolution fusion | flops 150994944 | bytes 2670592 | tf_op jit(solution)/shard_map/while/body/eval_jaxpr/cnybx,cnybz->nbxz/dot_general | solution.py:67
  357.8 9.1 %fusion.64 = f32[8,32,48]{2,1,0:T(8,128)S(1)} fusion(f32[32,1,32,8,32]{2,4,0,3,1:T(8,128)} %get-tuple-element.137, f32[32,32,8,48]{3,2,1,0:T(8,128)} %reshape.141), kind=kOutput, calls=%fused_computation.4.clone.1 | convolution fusion | flops 150994944 | bytes 2670592 | tf_op jit(solution)/shard_map/while/body/eval_jaxpr/cnybx,cnybz->nbxz/dot_general | solution.py:67
  374.7 9.1 %fusion.64 = f32[8,32,48]{2,1,0:T(8,128)S(1)} fusion(f32[32,1,32,8,32]{2,4,0,3,1:T(8,128)} %get-tuple-element.137, f32[32,32,8,48]{3,2,1,0:T(8,128)} %reshape.141), kind=kOutput, calls=%fused_computation.4.clone.1 | convolution fusion | flops 150994944 | bytes 2670592 | tf_op jit(solution)/shard_map/while/body/eval_jaxpr/cnybx,cnybz->nbxz/dot_general | solution.py:67
  391.6 9.1 %fusion.64 = f32[8,32,48]{2,1,0:T(8,128)S(1)} fusion(f32[32,1,32,8,32]{2,4,0,3,1:T(8,128)} %get-tuple-element.137, f32[32,32,8,48]{3,2,1,0:T(8,128)} %reshape.141), kind=kOutput, calls=%fused_computation.4.clone.1 | convolution fusion | flops 150994944 | bytes 2670592 | tf_op jit(solution)/shard_map/while/body/eval_jaxpr/cnybx,cnybz->nbxz/dot_general | solution.py:67
  408.5 9.1 %fusion.64 = f32[8,32,48]{2,1,0:T(8,128)S(1)} fusion(f32[32,1,32,8,32]{2,4,0,3,1:T(8,128)} %get-tuple-element.137, f32[32,32,8,48]{3,2,1,0:T(8,128)} %reshape.141), kind=kOutput, calls=%fused_computation.4.clone.1 | convolution fusion | flops 150994944 | bytes 2670592 | tf_op jit(solution)/shard_map/while/body/eval_jaxpr/cnybx,cnybz->nbxz/dot_general | solution.py:67
  425.4 9.1 %fusion.64 = f32[8,32,48]{2,1,0:T(8,128)S(1)} fusion(f32[32,1,32,8,32]{2,4,0,3,1:T(8,128)} %get-tuple-element.137, f32[32,32,8,48]{3,2,1,0:T(8,128)} %reshape.141), kind=kOutput, calls=%fused_computation.4.clone.1 | convolution fusion | flops 150994944 | bytes 2670592 | tf_op jit(solution)/shard_map/while/body/eval_jaxpr/cnybx,cnybz->nbxz/dot_general | solution.py:67
  442.3 9.1 %fusion.64 = f32[8,32,48]{2,1,0:T(8,128)S(1)} fusion(f32[32,1,32,8,32]{2,4,0,3,1:T(8,128)} %get-tuple-element.137, f32[32,32,8,48]{3,2,1,0:T(8,128)} %reshape.141), kind=kOutput, calls=%fused_computation.4.clone.1 | convolution fusion | flops 150994944 | bytes 2670592 | tf_op jit(solution)/shard_map/while/body/eval_jaxpr/cnybx,cnybz->nbxz/dot_general | solution.py:67
  459.2 9.1 %fusion.64 = f32[8,32,48]{2,1,0:T(8,128)S(1)} fusion(f32[32,1,32,8,32]{2,4,0,3,1:T(8,128)} %get-tuple-element.137, f32[32,32,8,48]{3,2,1,0:T(8,128)} %reshape.141), kind=kOutput, calls=%fused_computation.4.clone.1 | convolution fusion | flops 150994944 | bytes 2670592 | tf_op jit(solution)/shard_map/while/body/eval_jaxpr/cnybx,cnybz->nbxz/dot_general | solution.py:67
  476.0 9.1 %fusion.64 = f32[8,32,48]{2,1,0:T(8,128)S(1)} fusion(f32[32,1,32,8,32]{2,4,0,3,1:T(8,128)} %get-tuple-element.137, f32[32,32,8,48]{3,2,1,0:T(8,128)} %reshape.141), kind=kOutput, calls=%fused_computation.4.clone.1 | convolution fusion | flops 150994944 | bytes 2670592 | tf_op jit(solution)/shard_map/while/body/eval_jaxpr/cnybx,cnybz->nbxz/dot_general | solution.py:67
  492.9 9.1 %fusion.64 = f32[8,32,48]{2,1,0:T(8,128)S(1)} fusion(f32[32,1,32,8,32]{2,4,0,3,1:T(8,128)} %get-tuple-element.137, f32[32,32,8,48]{3,2,1,0:T(8,128)} %reshape.141), kind=kOutput, calls=%fused_computation.4.clone.1 | convolution fusion | flops 150994944 | bytes 2670592 | tf_op jit(solution)/shard_map/while/body/eval_jaxpr/cnybx,cnybz->nbxz/dot_general | solution.py:67
  509.7 9.1 %fusion.64 = f32[8,32,48]{2,1,0:T(8,128)S(1)} fusion(f32[32,1,32,8,32]{2,4,0,3,1:T(8,128)} %get-tuple-element.137, f32[32,32,8,48]{3,2,1,0:T(8,128)} %reshape.141), kind=kOutput, calls=%fused_computation.4.clone.1 | convolution fusion | flops 150994944 | bytes 2670592 | tf_op jit(solution)/shard_map/while/body/eval_jaxpr/cnybx,cnybz->nbxz/dot_general | solution.py:67
  (147 shorter events, 215.8 us)
Async XLA Ops:
  0.0 10.7 %copy-start = (f32[32,1,3,3]{0,1,3,2:T(1,128)S(1)}, f32[32,1,3,3]{0,1,3,2:T(1,128)}, u32[]{:S(2)}) copy-start(f32[32,1,3,3]{0,1,3,2:T(1,128)} %param.11) | copy-start | bytes 3460
  0.7 6.1 %collective-permute-start = (f32[1,1,256]{2,1,0:T(1,128)S(1)}, f32[1,1,256]{2,1,0:T(1,128)S(1)}, u32[]{:S(2)}, u32[]{:S(2)}) collective-permute-start(f32[1,1,256]{2,1,0:T(1,128)S(1)} %get-tuple-element.73), channel_id=1, source_target_pairs={{0,1},{1,2},{2,3},{4,5},{5,6},{6,7},{8,9},{9,10},{10,11},{12,13},{... | collective-permute-start | bytes 3080 | tf_op jit(solution)/shard_map/ppermute | solution.py:18
  4.8 4.3 collective-permute-start.1
  37.0 4.7 collective-permute-start.2
  40.2 4.7 collective-permute-start.3
  48.6 7.1 %copy-start.3 = (f32[2,32,32,3,3]{2,1,4,3,0:T(8,128)S(1)}, f32[2,32,32,3,3]{2,1,4,3,0:T(8,128)}, u32[]{:S(2)}) copy-start(f32[2,32,32,3,3]{2,1,4,3,0:T(8,128)} %param.12) | copy-start | bytes 221188
  48.6 7.2 %copy-start.5 = (pred[8,33]{0,1:T(8,128)(4,1)S(1)}, pred[8,33]{0,1:T(8,128)(4,1)}, u32[]{:S(2)}) copy-start(pred[8,33]{0,1:T(8,128)(4,1)} %constant.40) | copy-start | bytes 796
  104.0 4.7 collective-permute-start.4
  107.2 4.7 collective-permute-start.5
  167.1 15.3 %copy-start.4 = (s32[1,1,8]{2,1,0:T(1,128)S(1)}, s32[1,1,8]{2,1,0:T(1,128)}, u32[]{:S(2)}) copy-start(s32[1,1,8]{2,1,0:T(1,128)} %param.10) | copy-start | bytes 100
  171.8 20.0 %collective-permute-start.6 = (f32[32,32,256]{2,0,1:T(8,128)}, f32[32,32,256]{2,0,1:T(8,128)}, u32[]{:S(2)}, u32[]{:S(2)}) collective-permute-start(f32[32,32,256]{2,0,1:T(8,128)} %bitcast_add_fusion), channel_id=1, source_target_pairs={{0,4},{4,8},{8,12},{1,5},{5,9},{9,13},{2,6},{6,10},{10,14},{3,7},{... | collective-permute-start | bytes 3145736 | tf_op jit(solution)/shard_map/ppermute | solution.py:27
  179.8 16.4 %collective-permute-start.7 = (f32[32,32,256]{2,0,1:T(8,128)}, f32[32,32,256]{2,0,1:T(8,128)}, u32[]{:S(2)}, u32[]{:S(2)}) collective-permute-start(f32[32,32,256]{2,0,1:T(8,128)} %bitcast_add_fusion), channel_id=1, source_target_pairs={{4,0},{8,4},{12,8},{5,1},{9,5},{13,9},{6,2},{10,6},{14,10},{7,3},{... | collective-permute-start | bytes 3145736 | tf_op jit(solution)/shard_map/ppermute | solution.py:27
  190.7 10.3 %copy-start.2 = (f32[32,1,32,8,32]{2,4,0,3,1:T(8,128)S(1)}, f32[32,1,32,8,32]{2,4,0,3,1:T(8,128)}, u32[]{:S(2)}) copy-start(f32[32,1,32,8,32]{2,4,0,3,1:T(8,128)} %copy.46) | copy-start | bytes 3145732
  197.8 5.9 %collective-permute-start.8 = (f32[32,8,256]{2,0,1:T(8,128)S(1)}, f32[32,8,256]{2,0,1:T(8,128)S(1)}, u32[]{:S(2)}, u32[]{:S(2)}) collective-permute-start(f32[32,8,256]{2,0,1:T(8,128)S(1)} %get-tuple-element.67), channel_id=1, source_target_pairs={{0,1},{1,2},{2,3},{4,5},{5,6},{6,7},{8,9},{9,10},{10,11},{12,13},{... | collective-permute-start | bytes 786440 | tf_op jit(solution)/shard_map/ppermute | solution.py:18
  199.7 7.1 %collective-permute-start.9 = (f32[32,8,256]{2,0,1:T(8,128)S(1)}, f32[32,8,256]{2,0,1:T(8,128)S(1)}, u32[]{:S(2)}, u32[]{:S(2)}) collective-permute-start(f32[32,8,256]{2,0,1:T(8,128)S(1)} %get-tuple-element.68), channel_id=1, source_target_pairs={{1,0},{2,1},{3,2},{5,4},{6,5},{7,6},{9,8},{10,9},{11,10},{13,12},{... | collective-permute-start | bytes 786440 | tf_op jit(solution)/shard_map/ppermute | solution.py:19
  519.3 0.8 copy-start.1
where the time goes:
time: 528 us; the launch traced here: 521 us
  matrix products  257 us (49%)
  local copies, waits for them, and re-layouts  167 us (32%)
  loops' own time  32.4 us (6%)
  starting transfers between devices  27.7 us (5%)
  other arithmetic  17.4 us (3%)
  waiting for transfers between devices  17.1 us (3%)
    dot_general x17, matrix products, one_shift(): jnp.einsum('cnybx,cnybz->nbxz', blocks, strip_band, precision=lax.Precisi...  155 us
    conv_general_dilated x3, matrix products, apply_layer(): lax.conv_general_dilated(current[None], kernel, (1, 1), ((0, 0), (1, 1)),...  93.1 us
    another operation x17, local copies, waits for them, and re-layouts  50 us
    conv_general_dilated x16, local copies, waits for them, and re-layouts, apply_layer(): lax.conv_general_dilated(current[None], kernel, (1, 1), ((0, 0), (1, 1)),...  49.9 us
    another operation x1, loops' own time, correlate(): shifted = lax.map(one_shift, jnp.arange(2 * RADIUS + 1, dtype=jnp.int32))  32.4 us
    dynamic_slice x17, local copies, waits for them, and re-layouts, one_shift(): strip_band = lax.dynamic_slice_in_dim(windows, offset, strip_rows, 1)  30 us
    ppermute x4, starting transfers between devices, with_halo(): before = lax.ppermute(last, axis, up)  12.3 us
    ppermute x4, waiting for transfers between devices, with_halo(): after = lax.ppermute(first, axis, down)  11.6 us
  transfers between devices with their start and end apart: 10, of which 6 were waited for; matrix products, arithmetic and copies ran while one was open for 2% of the time, Pallas kernels for 0%

commit v1 on v0

v1 whole, which is shorter than its diff:
```python
import functools

import jax
import jax.numpy as jnp
import numpy as np
from jax import lax
from jax.experimental import pallas as pl
from jax.experimental.pallas import tpu as pltpu
from jax.sharding import PartitionSpec as P

LAYERS = 3
BLK = 32
RADIUS = 8
C = 32
SHIFTS = 2 * RADIUS + 1
HALO = RADIUS + LAYERS
RAW_ROWS = 64
GROUP = 6
LANES = 128
bf16 = jnp.bfloat16
f32 = jnp.float32


def pairs_even(n):
    return [(i, i ^ 1) for i in range(n) if (i ^ 1) < n]


def pairs_odd(n):
    return [(i, ((i + 1) ^ 1) - 1) for i in range(n) if 0 <= ((i + 1) ^ 1) - 1 < n]


def split(value):
    high = value.astype(bf16)
    return high, (value - high.astype(f32)).astype(bf16)


def dot(left, right):
    return jnp.dot(left, right, preferred_element_type=f32)


def kernel(
    info, own_ref, even_ref, odd_ref, wc_ref, bias_ref, out_ref,
    t1, t2h, t2l, t3h, t3l, raw, x1h, x1l, x2h, x2l, x3h, x3l, bh, bl, ah, al,
):
    width = 256
    iota = lambda shape, axis: lax.broadcasted_iota(jnp.int32, shape, axis)
    tile, tiles, section, pair = info[0], info[1], info[2], info[3]

    lane = iota((C, LANES), 1)
    first = wc_ref[2 * 96:2 * 96 + C, :]
    for yo in range(8):
        rolled = pltpu.roll(first, yo, 1) if yo else first
        high, low = split(rolled)
        rows = slice(yo * C, (yo + 1) * C)
        t1[rows, 0:48] = high[:, 0:48]
        t1[rows, 48:96] = low[:, 0:48]
        t1[rows, 96:144] = high[:, 0:48]
    for layer, (th, tl) in enumerate(((t2h, t2l), (t3h, t3l))):
        for kx in range(3):
            piece = wc_ref[layer * 96 + kx * C:layer * 96 + (kx + 1) * C, :]
            wide = jnp.concatenate([piece, jnp.zeros((C, LANES), f32)], axis=1)
            for yo in range(GROUP):
                rolled = pltpu.roll(wide, yo * C, 1) if yo else wide
                high, low = split(rolled)
                rows = slice((kx * GROUP + yo) * C, (kx * GROUP + yo + 1) * C)
                th[rows, :] = high
                tl[rows, :] = low

    own = own_ref[...]
    partner = jnp.where(pair == section, own, jnp.where(pair == (section ^ 1), even_ref[...], odd_ref[...]))
    col = iota((RAW_ROWS, width), 1)
    for which, image in enumerate((own, partner)):
        raw[which, 0] = jnp.where(col == 0, 0.0, pltpu.roll(image, 1, 1))
        raw[which, 1] = image
        raw[which, 2] = jnp.where(col == width - 1, 0.0, pltpu.roll(image, width - 1, 1))

    plan = ((0, 8, 5, 6, 6, 0, 0), (1, 0, 7, 9, 8, 0, 0))
    edge = iota((C, width), 1)

    def conv(th, tl, xh, xl, group, bias):
        rows = slice(group * GROUP * C, (group * GROUP + 8) * C)
        th, tl, xh, xl = th[...], tl[...], xh[rows, :], xl[rows, :]
        r = dot(jnp.concatenate([th, tl, th], 1), jnp.concatenate([xh, xh, xl], 0))
        n = GROUP * C
        outs = []
        for yo in range(GROUP):
            a = r[yo * C:(yo + 1) * C]
            b = r[n + yo * C:n + (yo + 1) * C]
            c = r[2 * n + yo * C:2 * n + (yo + 1) * C]
            a = jnp.where(edge == 0, 0.0, pltpu.roll(a, 1, 1))
            c = jnp.where(edge == width - 1, 0.0, pltpu.roll(c, width - 1, 1))
            outs.append(a + b + c + bias)
        return outs

    def zero(refs, first_row, last_row):
        for ref in refs:
            ref[first_row * C:last_row * C, :] = jnp.zeros(((last_row - first_row) * C, width), bf16)

    for which in range(2):
        if which == 0:
            base, g1, g2, g3 = 8, 5, 6, 6
            top1, top2, end1, end2 = 2, 1, 34, 33
            o3h, o3l = x3h, x3l
        else:
            base, g1, g2, g3 = 0, 7, 9, 8
            top1, top2, end1, end2 = 10, 9, 42, 41
            o3h, o3l = bh, bl
        bias1 = jnp.broadcast_to(bias_ref[0:C, 0:1], (C, width))
        bias2 = jnp.broadcast_to(bias_ref[0:C, 1:2], (C, width))
        bias3 = jnp.broadcast_to(bias_ref[0:C, 2:3], (C, width))
        for g in range(g1):
            parts = [raw[which, kx, base + 8 * g:base + 8 * g + 16, :] for kx in range(3)]
            high, low = split(jnp.concatenate(parts, 0))
            r = dot(t1[...], jnp.concatenate([high, high, low], 0))
            for yo in range(8):
                high, low = split(jnp.tanh(r[yo * C:(yo + 1) * C] + bias1))
                rows = slice((8 * g + yo) * C, (8 * g + yo + 1) * C)
                x1h[rows, :] = high
                x1l[rows, :] = low
        n1, n2 = 8 * g1, GROUP * g2

        @pl.when(tile == 0)
        def _():
            zero((x1h, x1l), 0, top1)

        @pl.when(tile == tiles - 1)
        def _():
            zero((x1h, x1l), end1, n1)

        for g in range(g2):
            for yo, value in enumerate(conv(t2h, t2l, x1h, x1l, g, bias2)):
                high, low = split(jnp.tanh(value))
                rows = slice((GROUP * g + yo) * C, (GROUP * g + yo + 1) * C)
                x2h[rows, :] = high
                x2l[rows, :] = low
        if which == 0:
            zero((x2h, x2l), 36, 38)

        @pl.when(tile == 0)
        def _():
            zero((x2h, x2l), 0, top2)

        @pl.when(tile == tiles - 1)
        def _():
            zero((x2h, x2l), end2, n2)

        for g in range(g3):
            for yo, value in enumerate(conv(t3h, t3l, x2h, x2l, g, bias3)):
                high, low = split(value)
                rows = slice((GROUP * g + yo) * C, (GROUP * g + yo + 1) * C)
                o3h[rows, :] = high
                o3l[rows, :] = low

    @pl.when(tile == 0)
    def _():
        zero((bh, bl), 0, 8)

    @pl.when(tile == tiles - 1)
    def _():
        zero((bh, bl), 40, 48)

    n = BLK * C
    ah[...] = jnp.transpose(x3h[0:n, :])
    al[...] = jnp.transpose(x3l[0:n, :])
    left = jnp.concatenate([ah[...], al[...], ah[...]], 1)
    lane8 = iota((8, LANES), 1)
    sub8 = iota((8, LANES), 0)
    weight = jnp.zeros((8, LANES), f32)
    for b in range(8):
        weight = jnp.where(sub8 == b, info[4 + b].astype(f32), weight)
    weight = weight * np.float32(1.0 / np.sqrt(BLK * BLK * C))
    total = jnp.zeros((8, 3 * LANES), f32)
    for dy in range(SHIFTS):
        rows = slice(dy * C, dy * C + n)
        high = bh[rows, :]
        p = dot(left, jnp.concatenate([high, high, bl[rows, :]], 0))
        sums = []
        for b in range(8):
            acc = None
            for j in range(4):
                start = BLK * b - RADIUS + 8 * j
                v = p[BLK * b + 8 * j:BLK * b + 8 * j + 8, :]
                v = pltpu.roll(v, (width - start) % width, 1)[:, :LANES] if start else v[:, :LANES]
                if start < 0:
                    v = jnp.where(lane8 < -start, 0.0, v)
                if start + 24 > width:
                    v = jnp.where(lane8 >= width - start, 0.0, v)
                acc = v if acc is None else acc + v
            for bit in (1, 2, 4):
                acc = jnp.where((sub8 & bit) != 0, pltpu.roll(acc, LANES - bit, 1), acc)
            sums.append(jnp.sum(acc, axis=0, keepdims=True))
        d = jnp.where(lane8 < SHIFTS, jnp.concatenate(sums, 0), 0.0)
        d = jnp.concatenate([d, jnp.zeros((8, 2 * LANES), f32)], 1)
        total = total + (pltpu.roll(d, SHIFTS * dy, 1) if dy else d)
    total = total * jnp.concatenate([weight] * 3, 1)
    out_ref[...] = total[:, :SHIFTS * SHIFTS]


def call_kernel(info, own, even, odd, compact, bias):
    width = own.shape[-1]
    vmem = pl.BlockSpec(memory_space=pltpu.VMEM)
    buf = lambda rows: pltpu.VMEM((rows * C, width), bf16)
    return pl.pallas_call(
        kernel,
        out_shape=jax.ShapeDtypeStruct((8, SHIFTS * SHIFTS), f32),
        in_specs=[pl.BlockSpec(memory_space=pltpu.SMEM)] + [vmem] * 5,
        out_specs=vmem,
        scratch_shapes=[
            pltpu.VMEM((256, 144), bf16),
            pltpu.VMEM((576, 256), bf16), pltpu.VMEM((576, 256), bf16),
            pltpu.VMEM((576, 256), bf16), pltpu.VMEM((576, 256), bf16),
            pltpu.VMEM((2, 3, RAW_ROWS, width), f32),
            buf(56), buf(56), buf(54), buf(54), buf(36), buf(36), buf(48), buf(48),
            pltpu.VMEM((width, BLK * C), bf16), pltpu.VMEM((width, BLK * C), bf16),
        ],
        compiler_params=pltpu.CompilerParams(vmem_limit_bytes=48 << 20),
        name="correlate",
    )(info, own, even, odd, compact, bias)


def body(raw_image, pairing, valid_mask, first_kernel, later_kernels, biases):
    tiles, sections = lax.axis_size("tile"), lax.axis_size("sec")
    tile, section = lax.axis_index("tile"), lax.axis_index("sec")
    image = raw_image[0]
    rows, width = image.shape
    odd_tile = (tile % 2) == 1
    top, bottom = image[:HALO], image[rows - HALO:]
    got_even = lax.ppermute(jnp.where(odd_tile, top, bottom), "tile", pairs_even(tiles))
    got_odd = lax.ppermute(jnp.where(odd_tile, bottom, top), "tile", pairs_odd(tiles))
    above = jnp.where(odd_tile, got_even, got_odd)
    below = jnp.where(odd_tile, got_odd, got_even)
    own = jnp.concatenate([above, image, below, jnp.zeros((RAW_ROWS - rows - 2 * HALO, width), f32)], 0)
    even = lax.ppermute(own, "sec", pairs_even(sections))
    odd = lax.ppermute(own, "sec", pairs_odd(sections))

    later = jnp.transpose(later_kernels, (0, 4, 1, 3, 2)).reshape(2 * 3 * C, 3 * C)
    later = jnp.pad(later, ((0, 0), (0, LANES - 3 * C)))
    first = jnp.pad(jnp.transpose(first_kernel[:, 0], (0, 2, 1)), ((0, 0), (0, 0), (0, 13))).reshape(C, 48)
    first = jnp.pad(first, ((0, 0), (0, LANES - 48)))
    compact = jnp.concatenate([later, first], 0)
    info = jnp.concatenate([
        jnp.stack([tile, jnp.int32(tiles), section, pairing[0]]).astype(jnp.int32),
        valid_mask.reshape(-1),
    ])
    result = call_kernel(info, own, even, odd, compact, jnp.transpose(biases))
    return result[None, None]


def solution(mesh):
    placed = (
        P(("groups", "sec"), "tile", None),
        P(("groups", "sec")),
        P(("groups", "sec"), "tile", None),
        P(),
        P(),
        P(),
    )
    return jax.shard_map(
        body,
        mesh=mesh,
        in_specs=placed,
        out_specs=P(("groups", "sec"), "tile", None, None),
        check_vma=False,
    )
```

time: 528 us -> 35.8 us (0.07)
  the two profiles are of different devices: /device:TPU:1 before, /device:TPU:13 now
where the time goes in v1:
time: 35.8 us; the launch traced here: 35.4 us
  Pallas kernels  18.4 us (51%)
  starting transfers between devices  8.75 us (24%)
  local copies, waits for them, and re-layouts  4.18 us (12%)
  waiting for transfers between devices  2.52 us (7%)
  other arithmetic  0.84 us (2%)
  between operations  0.72 us (2%)
    pallas_call x1, Pallas kernels, call_kernel(): pl.pallas_call(kernel, out_shape=jax.ShapeDtypeStruct((8, SHIFTS * SHIFTS...  18.4 us
    ppermute x1, starting transfers between devices, body(): lax.ppermute(jnp.where(odd_tile, bottom, top), 'tile', pairs_odd(tiles))  4.32 us
    ppermute x1, starting transfers between devices, body(): odd = lax.ppermute(own, 'sec', pairs_odd(sections))  3.02 us
    unnamed x9, local copies, waits for them, and re-layouts  2.58 us
    ppermute x1, waiting for transfers between devices, body(): odd = lax.ppermute(own, 'sec', pairs_odd(sections))  2.52 us
    ppermute x1, starting transfers between devices, body(): even = lax.ppermute(own, 'sec', pairs_even(sections))  1.24 us
    transpose x1, local copies, waits for them, and re-layouts, body(): jnp.transpose(later_kernels, (0, 4, 1, 3, 2)).reshape(2 * 3 * C, 3 * C)  1.17 us
    select_n x1, other arithmetic, body(): jnp.where(odd_tile, top, bottom)  0.74 us
  transfers between devices with their start and end apart: 4, of which 1 were waited for; matrix products, arithmetic and copies ran while one was open for 5% of the time, Pallas kernels for 0%

profile of v1, /device:TPU:13, one launch (start us, length us, event | category | flops | bytes accessed | tf_op | source)
XLA Modules:
  0.0 35.4 jit_solution(13348289764836931789)
XLA Ops:
  0.0 0.7 %select_bitcast_fusion.1 = (f32[11,256]{1,0:T(8,128)S(1)}, f32[11,256]{1,0:T(8,128)S(1)}) fusion(f32[1,32,256]{2,1,0:T(8,128)} %param.6, pred[]{:T(512)S(6)} %eq.5), kind=kLoop, calls=%fused_computation.5 | loop fusion | flops 5632 | bytes 45057 | tf_op jit(solution)/shard_map/jit(_where)/select_n | solution.py:228
  0.7 0.2 collective-permute-start
  0.9 4.3 %collective-permute-start.1 = (f32[11,256]{1,0:T(8,128)S(1)}, f32[11,256]{1,0:T(8,128)S(1)}, u32[]{:S(2)}, u32[]{:S(2)}) collective-permute-start(f32[11,256]{1,0:T(8,128)S(1)} %get-tuple-element.8), channel_id=1, source_target_pairs={{1,2},{2,1},{5,6},{6,5},{9,10},{10,9},{13,14},{14,13},{17,18},{18,... | collective-permute-start | bytes 33800 | tf_op jit(solution)/shard_map/ppermute | solution.py:229
  5.9 1.2 %copy.10 = f32[2,3,32,3,32]{4,3,2,1,0:T(4,128)S(1)} copy(f32[2,3,32,3,32]{4,2,1,3,0:T(8,128)} %bitcast.19) | data formatting | bytes 147456 | tf_op jit(solution)/shard_map/transpose | solution.py:236
  7.1 0.0 copy-start.1
  7.1 0.2 reshape.16
  7.3 0.5 %copy-done.1 = f32[32,1,3,3]{0,1,3,2:T(1,128)S(1)} copy-done((f32[32,1,3,3]{0,1,3,2:T(1,128)S(1)}, f32[32,1,3,3]{0,1,3,2:T(1,128)}, u32[]{:S(2)}) %copy-start.1) | copy-done | bytes 1176
  7.8 0.0 copy-start.2
  7.8 0.1 copy.12
  7.8 0.6 %copy-done.2 = f32[3,32]{1,0:T(4,128)S(1)} copy-done((f32[3,32]{1,0:T(4,128)S(1)}, f32[3,32]{1,0:T(4,128)}, u32[]{:S(2)}) %copy-start.2) | copy-done | bytes 408
  8.5 0.1 copy.13
  8.5 0.1 pad.20.clone
  8.6 0.0 copy-start.3
  8.6 0.7 %copy-done.3 = s32[1,1,8]{2,1,0:T(1,128)S(1)} copy-done((s32[1,1,8]{2,1,0:T(1,128)S(1)}, s32[1,1,8]{2,1,0:T(1,128)}, u32[]{:S(2)}) %copy-start.3) | copy-done | bytes 56
  9.3 0.1 concatenate.9.info
  9.4 0.0 collective-permute-done
  9.4 0.0 collective-permute-done.1
  9.4 0.7 %copy-done = f32[1,32,256]{2,1,0:T(8,128)S(1)} copy-done((f32[1,32,256]{2,1,0:T(8,128)S(1)}, f32[1,32,256]{2,1,0:T(8,128)}, u32[]{:S(2)}) %copy-start) | copy-done | bytes 32792
  10.1 0.1 maximum_maximum_fusion.own_ref
  10.2 1.2 %collective-permute-start.2 = (f32[64,256]{1,0:T(8,128)S(1)}, f32[64,256]{1,0:T(8,128)S(1)}, u32[]{:S(2)}, u32[]{:S(2)}) collective-permute-start(f32[64,256]{1,0:T(8,128)S(1)} %maximum_maximum_fusion.own_ref), channel_id=1, source_target_pairs={{0,4},{4,0},{8,12},{12,8},{1,5},{5,1},{9,13},{13,9},{2,6},{6,2},{1... | collective-permute-start | bytes 196616 | tf_op jit(solution)/shard_map/ppermute | solution.py:233
  11.4 3.0 %collective-permute-start.3 = (f32[64,256]{1,0:T(8,128)S(1)}, f32[64,256]{1,0:T(8,128)S(1)}, u32[]{:S(2)}, u32[]{:S(2)}) collective-permute-start(f32[64,256]{1,0:T(8,128)S(1)} %maximum_maximum_fusion.own_ref), channel_id=1, source_target_pairs={{4,8},{8,4},{5,9},{9,5},{6,10},{10,6},{7,11},{11,7},{20,24},{24,20... | collective-permute-start | bytes 196616 | tf_op jit(solution)/shard_map/ppermute | solution.py:234
  14.5 0.0 collective-permute-done.2.even_ref
  14.5 2.5 %collective-permute-done.3.odd_ref = f32[64,256]{1,0:T(8,128)S(1)} collective-permute-done((f32[64,256]{1,0:T(8,128)S(1)}, f32[64,256]{1,0:T(8,128)S(1)}, u32[]{:S(2)}, u32[]{:S(2)}) %collective-permute-start.3) | collective-permute-done | bytes 65568 | tf_op jit(solution)/shard_map/ppermute | solution.py:234
  17.0 18.4 %correlate.1 = f32[8,289]{1,0:T(8,128)} custom-call(s32[12]{0:T(128)S(1)} %concatenate.9.info, f32[64,256]{1,0:T(8,128)S(1)} %maximum_maximum_fusion.own_ref, f32[64,256]{1,0:T(8,128)S(1)} %collective-permute-done.2.even_ref, f32[64,256]{1,0:T(8,128)S(1)} %collective-permute-done.3.odd_ref, f32[224,128]{1,0:T(8,128)S(1)} %select_maximum_fusion.wc_ref, ...), custom_call_target="tpu_custom_call" | custom-call | tf_op jit(solution)/shard_map/correlate/pallas_call | solution.py:203
  (6 shorter events, 0.0 us)
Async XLA Ops:
  0.7 8.6 %collective-permute-start = (f32[11,256]{1,0:T(8,128)S(1)}, f32[11,256]{1,0:T(8,128)S(1)}, u32[]{:S(2)}, u32[]{:S(2)}) collective-permute-start(f32[11,256]{1,0:T(8,128)S(1)} %get-tuple-element.7), channel_id=1, source_target_pairs={{0,1},{1,0},{2,3},{3,2},{4,5},{5,4},{6,7},{7,6},{8,9},{9,8},{10,11... | collective-permute-start | bytes 33800 | tf_op jit(solution)/shard_map/ppermute | solution.py:228
  0.9 8.5 %collective-permute-start.1 = (f32[11,256]{1,0:T(8,128)S(1)}, f32[11,256]{1,0:T(8,128)S(1)}, u32[]{:S(2)}, u32[]{:S(2)}) collective-permute-start(f32[11,256]{1,0:T(8,128)S(1)} %get-tuple-element.8), channel_id=1, source_target_pairs={{1,2},{2,1},{5,6},{6,5},{9,10},{10,9},{13,14},{14,13},{17,18},{18,... | collective-permute-start | bytes 33800 | tf_op jit(solution)/shard_map/ppermute | solution.py:229
  7.1 0.7 %copy-start.1 = (f32[32,1,3,3]{0,1,3,2:T(1,128)S(1)}, f32[32,1,3,3]{0,1,3,2:T(1,128)}, u32[]{:S(2)}) copy-start(f32[32,1,3,3]{0,1,3,2:T(1,128)} %param.9) | copy-start | bytes 3460
  7.8 0.7 %copy-start.2 = (f32[3,32]{1,0:T(4,128)S(1)}, f32[3,32]{1,0:T(4,128)}, u32[]{:S(2)}) copy-start(f32[3,32]{1,0:T(4,128)} %param.11) | copy-start | bytes 1156
  8.6 0.7 %copy-start.3 = (s32[1,1,8]{2,1,0:T(1,128)S(1)}, s32[1,1,8]{2,1,0:T(1,128)}, u32[]{:S(2)}) copy-start(s32[1,1,8]{2,1,0:T(1,128)} %param.8) | copy-start | bytes 100
  9.4 0.8 %copy-start = (f32[1,32,256]{2,1,0:T(8,128)S(1)}, f32[1,32,256]{2,1,0:T(8,128)}, u32[]{:S(2)}) copy-start(f32[1,32,256]{2,1,0:T(8,128)} %param.6) | copy-start | bytes 98308
  10.2 4.3 %collective-permute-start.2 = (f32[64,256]{1,0:T(8,128)S(1)}, f32[64,256]{1,0:T(8,128)S(1)}, u32[]{:S(2)}, u32[]{:S(2)}) collective-permute-start(f32[64,256]{1,0:T(8,128)S(1)} %maximum_maximum_fusion.own_ref), channel_id=1, source_target_pairs={{0,4},{4,0},{8,12},{12,8},{1,5},{5,1},{9,13},{13,9},{2,6},{6,2},{1... | collective-permute-start | bytes 196616 | tf_op jit(solution)/shard_map/ppermute | solution.py:233
  11.4 5.6 %collective-permute-start.3 = (f32[64,256]{1,0:T(8,128)S(1)}, f32[64,256]{1,0:T(8,128)S(1)}, u32[]{:S(2)}, u32[]{:S(2)}) collective-permute-start(f32[64,256]{1,0:T(8,128)S(1)} %maximum_maximum_fusion.own_ref), channel_id=1, source_target_pairs={{4,8},{8,4},{5,9},{9,5},{6,10},{10,6},{7,11},{11,7},{20,24},{24,20... | collective-permute-start | bytes 196616 | tf_op jit(solution)/shard_map/ppermute | solution.py:234

commit v2 on v0

v2 whole, which is shorter than its diff:
```python
import jax
import jax.numpy as jnp
import numpy as np
from jax import lax
from jax.experimental import pallas as pl
from jax.experimental.pallas import tpu as pltpu
from jax.sharding import PartitionSpec as P

LAYERS = 3
BLK = 32
RADIUS = 8
C = 32
SHIFTS = 2 * RADIUS + 1
HALO = RADIUS + LAYERS
RAW_ROWS = 64
GROUP = 6
LANES = 128
WIDTH = 256
WIN = 64
SPAN = WIN + 2 * RADIUS
JOINT = 4
STEPS = 5
DEEP = (BLK + JOINT) * C
BAND = 24
bf16 = jnp.bfloat16
f32 = jnp.float32


def pairs_even(n):
    return [(i, i ^ 1) for i in range(n) if (i ^ 1) < n]


def pairs_odd(n):
    return [(i, ((i + 1) ^ 1) - 1) for i in range(n) if 0 <= ((i + 1) ^ 1) - 1 < n]


def split(value):
    high = value.astype(bf16)
    return high, (value - high.astype(f32)).astype(bf16)


def dot(left, right):
    return jnp.dot(left, right, preferred_element_type=f32)


def iota(shape, axis):
    return lax.broadcasted_iota(jnp.int32, shape, axis)


def prepare(later_ref, first_ref, bias_ref, image_ref, t1, t2, t3, spread, image):
    image[...] = image_ref[...]
    for layer, t in enumerate((t2, t3)):
        for kx in range(3):
            taps = [later_ref[layer, ky, kx] for ky in range(3)]
            wide = jnp.concatenate(taps + [jnp.zeros((C, LANES - 3 * C), f32)], axis=1)
            wide = jnp.concatenate([wide, jnp.zeros((C, LANES), f32)], axis=1)
            for yo in range(GROUP):
                high, low = split(pltpu.roll(wide, yo * C, 1) if yo else wide)
                rows = slice((kx * GROUP + yo) * C, (kx * GROUP + yo + 1) * C)
                t[0, rows, :] = high
                t[1, rows, :] = low
    taps = first_ref[...]
    taps = jnp.concatenate([taps] * (WIDTH // C), axis=1)
    offset = iota((16, WIDTH), 0) - iota((16, WIDTH), 1) // C
    pieces = []
    for kx in range(3):
        piece = jnp.zeros((16, WIDTH), f32)
        for ky in range(3):
            row = taps[3 * ky + kx:3 * ky + kx + 1, :]
            piece = jnp.where(offset == ky, jnp.broadcast_to(row, (16, WIDTH)), piece)
        pieces.append(piece)
    pieces.append(jnp.zeros((LANES - 48, WIDTH), f32))
    high, low = split(jnp.transpose(jnp.concatenate(pieces, 0)))
    t1[:, 0:48] = high[:, 0:48]
    t1[:, 48:96] = low[:, 0:48]
    t1[:, 96:144] = high[:, 0:48]
    b = jnp.concatenate([bias_ref[...], jnp.zeros((LAYERS, LANES - C), f32)], 1)
    b = jnp.transpose(jnp.concatenate([b, jnp.zeros((8 - LAYERS, LANES), f32)], 0))
    for layer in range(LAYERS):
        spread[layer] = jnp.broadcast_to(b[0:C, layer:layer + 1], (C, WIDTH))


def encode(image, base, groups, ends, tile, tiles, t1, t2, t3, spread, raw, x1, x2, emit):
    n1, n2 = 8 * groups[0], GROUP * groups[1]
    col = iota((RAW_ROWS, WIDTH), 1)
    raw[0] = jnp.where(col == 0, 0.0, pltpu.roll(image, 1, 1))
    raw[1] = image
    raw[2] = jnp.where(col == WIDTH - 1, 0.0, pltpu.roll(image, WIDTH - 1, 1))
    edge = iota((C, WIDTH), 1)

    def put(x, row, value):
        high, low = split(value)
        x[0, row * C:(row + 1) * C, :] = high
        x[1, row * C:(row + 1) * C, :] = low

    def outside(x, top, end, rows):
        @pl.when(tile == 0)
        def _():
            x[:, 0:top * C, :] = jnp.zeros((2, top * C, WIDTH), bf16)

        @pl.when(tile == tiles - 1)
        def _():
            x[:, end * C:rows * C, :] = jnp.zeros((2, (rows - end) * C, WIDTH), bf16)

    def conv(t, x, group, bias):
        rows = slice(group * GROUP * C, (group * GROUP + 8) * C)
        th, tl, xh, xl = t[0], t[1], x[0, rows, :], x[1, rows, :]
        r = dot(jnp.concatenate([th, tl, th], 1), jnp.concatenate([xh, xh, xl], 0))
        n = GROUP * C
        for yo in range(GROUP):
            a = r[yo * C:(yo + 1) * C]
            b = r[n + yo * C:n + (yo + 1) * C]
            c = r[2 * n + yo * C:2 * n + (yo + 1) * C]
            a = jnp.where(edge == 0, 0.0, pltpu.roll(a, 1, 1))
            c = jnp.where(edge == WIDTH - 1, 0.0, pltpu.roll(c, WIDTH - 1, 1))
            yield group * GROUP + yo, a + b + c + bias

    for g in range(groups[0]):
        parts = [raw[kx, base + 8 * g:base + 8 * g + 16, :] for kx in range(3)]
        high, low = split(jnp.concatenate(parts, 0))
        r = dot(t1[...], jnp.concatenate([high, high, low], 0))
        for yo in range(8):
            put(x1, 8 * g + yo, jnp.tanh(r[yo * C:(yo + 1) * C] + spread[0]))
    outside(x1, ends[0], ends[1], n1)
    for g in range(groups[1]):
        for row, value in conv(t2, x1, g, spread[1]):
            put(x2, row, jnp.tanh(value))
    outside(x2, ends[2], ends[3], n2)
    for row in range(n2, GROUP * groups[2] + 2):
        x2[:, row * C:(row + 1) * C, :] = jnp.zeros((2, C, WIDTH), bf16)
    for g in range(groups[2]):
        for row, value in conv(t3, x2, g, spread[2]):
            emit(row, value)


def own_features(where, image_ref, t1, t2, t3, spread, packed, raw, x1, x2, kept):
    tile, tiles = where[0], where[1]
    pad = JOINT - 1
    kept[:, :, 0:pad * C, :] = jnp.zeros((2, 2, pad * C, WIDTH), bf16)
    kept[:, :, (pad + BLK) * C:, :] = jnp.zeros((2, 2, JOINT * C, WIDTH), bf16)

    def emit(row, value):
        if row >= BLK:
            return
        turned = [pltpu.roll(value[:, i:i + LANES], WIN, 1) for i in range(0, WIDTH, LANES)]
        rows = slice((row + pad) * C, (row + pad + 1) * C)
        for form, v in enumerate((value, jnp.concatenate(turned, 1))):
            kept[form, 0, rows, :], kept[form, 1, rows, :] = split(v)

    encode(image_ref[...], RADIUS, (5, 6, 6), (2, 34, 1, 33), tile, tiles,
           t1, t2, t3, spread, raw, x1, x2, emit)
    left = iota((C, LANES), 1) < WIN
    for w in range(WIDTH // WIN):
        half = slice((w // 2) * LANES, (w // 2 + 1) * LANES)
        for part in range(2):
            for y in range(BLK + JOINT):
                cols = []
                for g in (0, 2):
                    a = kept[w % 2, part, (y - g + pad) * C:(y - g + pad + 1) * C, half]
                    b = kept[1 - w % 2, part, (y - g - 1 + pad) * C:(y - g + pad) * C, half]
                    cols.append(jnp.where(left, a, b))
                packed[w, part, y * C:(y + 1) * C, :] = jnp.concatenate(cols, 1)


def correlate(where, pair, mask, own_ref, even_ref, odd_ref, t1, t2, t3, spread, packed, out_ref,
              raw, x1, x2, feats, turned):
    tile, tiles, section = where[0], where[1], where[2]
    image = jnp.where(pair[0] == section, own_ref[...],
                      jnp.where(pair[0] == (section ^ 1), even_ref[...], odd_ref[...]))

    def emit(row, value):
        feats[row * C:(row + 1) * C, :] = value

    encode(image, 0, (7, 9, 8), (10, 42, 9, 41), tile, tiles, t1, t2, t3, spread, raw, x1, x2, emit)

    @pl.when(tile == 0)
    def _():
        feats[0:RADIUS * C, :] = jnp.zeros((RADIUS * C, WIDTH), f32)

    @pl.when(tile == tiles - 1)
    def _():
        feats[(BLK + RADIUS) * C:, :] = jnp.zeros((RADIUS * C, WIDTH), f32)

    border = jnp.zeros((RADIUS, LANES), f32)
    turned[:, :, (BLK + 2 * RADIUS) * C:] = jnp.zeros((2, WIDTH + 2 * RADIUS, JOINT * C), bf16)
    for q in range((BLK + 2 * RADIUS) * C // LANES):
        cols = slice(q * LANES, (q + 1) * LANES)
        v = jnp.concatenate([border, jnp.transpose(feats[cols, :]), border], 0)
        turned[0, :, cols], turned[1, :, cols] = split(v)

    lane8, sub8 = iota((8, LANES), 1), iota((8, LANES), 0)
    eighth = (iota((8, WIDTH), 1) % WIN) // 8
    sums = [[None] * 8 for _ in range(JOINT)]
    for w in range(WIDTH // WIN):
        rows = slice(w * WIN, w * WIN + SPAN)
        lefts = []
        for j in range(STEPS):
            cols = slice(j * JOINT * C, j * JOINT * C + DEEP)
            high, low = turned[0, rows, cols], turned[1, rows, cols]
            lefts.append(jnp.concatenate([high, low, high], 1))
        right = jnp.concatenate([packed[w, 0], packed[w, 0], packed[w, 1]], 0)
        p = dot(jnp.concatenate(lefts, 0), right)
        bands = []
        for j in range(STEPS):
            for k in range(3):
                band = None
                for m in range(8):
                    start = j * SPAN + 8 * (m + k)
                    v = p[start:start + 8, :]
                    band = v if band is None else jnp.where(eighth == m, v, band)
                bands.append(band)
        bands.append(jnp.zeros((8, WIDTH), f32))
        flat = jnp.transpose(jnp.concatenate(bands, 0))
        for g in range(JOINT):
            for side in range(2):
                at = g * WIN + side * BLK
                v = flat[at:at + 8] + flat[at + 8:at + 16] + flat[at + 16:at + 24] + flat[at + 24:at + 32]
                for bit in (1, 2, 4):
                    v = jnp.where((sub8 & bit) != 0, pltpu.roll(v, LANES - bit, 1), v)
                sums[g][2 * w + side] = jnp.sum(v, axis=0, keepdims=True)
    total = jnp.zeros((8, 3 * LANES), f32)
    lane = iota((8, 3 * LANES), 1)
    for g in range(JOINT):
        d = jnp.concatenate(sums[g], 0)
        d = jnp.concatenate([d, jnp.zeros((8, 2 * LANES), f32)], 1)
        for j in range(STEPS):
            dy = JOINT * j + g
            if dy < SHIFTS:
                shift = (SHIFTS * dy - BAND * j) % (3 * LANES)
                here = (lane >= SHIFTS * dy) & (lane < SHIFTS * (dy + 1))
                total = jnp.where(here, pltpu.roll(d, shift, 1) if shift else d, total)
    weight = jnp.zeros((8, 3 * LANES), f32)
    for b in range(8):
        weight = jnp.where(iota((8, 3 * LANES), 0) == b, mask[b].astype(f32), weight)
    total = total * (weight * np.float32(1.0 / np.sqrt(BLK * BLK * C)))
    out_ref[...] = total[:, :SHIFTS * SHIFTS]


VMEM = pl.BlockSpec(memory_space=pltpu.VMEM)
SMEM = pl.BlockSpec(memory_space=pltpu.SMEM)


def params(flops, moved):
    return dict(
        compiler_params=pltpu.CompilerParams(vmem_limit_bytes=40 << 20),
        cost_estimate=pl.CostEstimate(flops=flops, bytes_accessed=moved, transcendentals=0),
    )


def scratch(rows1, rows2):
    return [
        pltpu.VMEM((3, RAW_ROWS, WIDTH), f32),
        pltpu.VMEM((2, rows1 * C, WIDTH), bf16),
        pltpu.VMEM((2, rows2 * C, WIDTH), bf16),
    ]


def body(raw_image, pairing, valid_mask, first_kernel, later_kernels, biases):
    tiles, sections = lax.axis_size("tile"), lax.axis_size("sec")
    tile, section = lax.axis_index("tile"), lax.axis_index("sec")
    image = raw_image[0]
    rows, width = image.shape
    shape = jax.ShapeDtypeStruct
    got_even = lax.ppermute(image, "tile", pairs_even(tiles))
    got_odd = lax.ppermute(image, "tile", pairs_odd(tiles))
    t1, t2, t3, spread, image = pl.pallas_call(
        prepare,
        out_shape=[shape((256, 144), bf16), shape((2, 576, 256), bf16), shape((2, 576, 256), bf16),
                   shape((LAYERS, C, WIDTH), f32), shape(image.shape, f32)],
        in_specs=[VMEM] * 4, out_specs=[VMEM] * 5, name="prepare", **params(10**6, 3 * 10**6),
    )(jnp.transpose(later_kernels, (0, 3, 4, 1, 2)),
      jnp.transpose(first_kernel, (2, 3, 1, 0)).reshape(9, C), biases, image)

    odd_tile = (tile % 2) == 1
    above = jnp.where(odd_tile, got_even[rows - HALO:], got_odd[rows - HALO:])
    below = jnp.where(odd_tile, got_odd[:HALO], got_even[:HALO])
    own = jnp.concatenate([above, image, below, jnp.zeros((RAW_ROWS - rows - 2 * HALO, width), f32)], 0)
    even = lax.ppermute(own, "sec", pairs_even(sections))
    odd = lax.ppermute(own, "sec", pairs_odd(sections))
    where = jnp.stack([tile, jnp.int32(tiles), section]).astype(jnp.int32)
    packed = pl.pallas_call(
        own_features,
        out_shape=shape((WIDTH // WIN, 2, DEEP, WIDTH), bf16),
        in_specs=[SMEM] + [VMEM] * 5, out_specs=VMEM,
        scratch_shapes=scratch(40, 38) + [pltpu.VMEM((2, 2, (BLK + 2 * JOINT - 1) * C, WIDTH), bf16)],
        name="own_features", **params(5 * 10**9, 10**7),
    )(where, own, t1, t2, t3, spread)
    result = pl.pallas_call(
        correlate,
        out_shape=shape((8, SHIFTS * SHIFTS), f32),
        in_specs=[SMEM] * 3 + [VMEM] * 8, out_specs=VMEM,
        scratch_shapes=scratch(56, 54) + [
            pltpu.VMEM(((BLK + 2 * RADIUS) * C, WIDTH), f32),
            pltpu.VMEM((2, WIDTH + 2 * RADIUS, (BLK + 2 * RADIUS + JOINT) * C), bf16),
        ],
        name="correlate", **params(10**10, 10**7),
    )(where, pairing, valid_mask.reshape(-1), own, even, odd, t1, t2, t3, spread, packed)
    return result[None, None]


def solution(mesh):
    placed = (
        P(("groups", "sec"), "tile", None),
        P(("groups", "sec")),
        P(("groups", "sec"), "tile", None),
        P(),
        P(),
        P(),
    )
    return jax.shard_map(
        body,
        mesh=mesh,
        in_specs=placed,
        out_specs=P(("groups", "sec"), "tile", None, None),
        check_vma=False,
    )
```

time: 528 us -> 29.9 us (0.06)
  the two profiles are of different devices: /device:TPU:1 before, /device:TPU:0 now
where the time goes in v2:
time: 29.9 us; the launch traced here: 29.6 us
  Pallas kernels  15.9 us (53%)
  starting transfers between devices  10.3 us (34%)
  local copies, waits for them, and re-layouts  2.52 us (8%)
  between operations  0.75 us (3%)
    pallas_call x1, Pallas kernels, body(): pl.pallas_call(correlate, out_shape=shape((8, SHIFTS * SHIFTS), f32), in_...  10.2 us
    ppermute x1, starting transfers between devices, body(): got_even = lax.ppermute(image, 'tile', pairs_even(tiles))  5.91 us
    pallas_call x1, Pallas kernels, body(): pl.pallas_call(own_features, out_shape=shape((WIDTH // WIN, 2, DEEP, WIDT...  5.01 us
    ppermute x1, starting transfers between devices, body(): even = lax.ppermute(own, 'sec', pairs_even(sections))  2.92 us
    unnamed x10, local copies, waits for them, and re-layouts  2.41 us
    ppermute x1, starting transfers between devices, body(): got_odd = lax.ppermute(image, 'tile', pairs_odd(tiles))  0.78 us
    pallas_call x1, Pallas kernels, body(): pl.pallas_call(prepare, out_shape=[shape((256, 144), bf16), shape((2, 576...  0.7 us
    ppermute x1, starting transfers between devices, body(): odd = lax.ppermute(own, 'sec', pairs_odd(sections))  0.65 us
  transfers between devices with their start and end apart: 4, of which 0 were waited for; matrix products, arithmetic and copies ran while one was open for 1% of the time, Pallas kernels for 19%

profile of v2, /device:TPU:0, one launch (start us, length us, event | category | flops | bytes accessed | tf_op | source)
XLA Modules:
  0.0 29.6 jit_solution(8332372731061259776)
XLA Ops:
  0.0 0.0 copy-start
  0.0 0.8 %collective-permute-start.1 = (f32[32,256]{1,0:T(8,128)}, f32[32,256]{1,0:T(8,128)S(1)}, u32[]{:S(2)}, u32[]{:S(2)}) collective-permute-start(f32[32,256]{1,0:T(8,128)} %bitcast.9), channel_id=1, source_target_pairs={{1,2},{2,1},{5,6},{6,5},{9,10},{10,9},{13,14},{14,13},{17,18},{18,... | collective-permute-start | bytes 98312 | tf_op jit(solution)/shard_map/ppermute | solution.py:265
  0.8 5.9 %collective-permute-start = (f32[32,256]{1,0:T(8,128)}, f32[32,256]{1,0:T(8,128)S(1)}, u32[]{:S(2)}, u32[]{:S(2)}) collective-permute-start(f32[32,256]{1,0:T(8,128)} %bitcast.10), channel_id=1, source_target_pairs={{0,1},{1,0},{2,3},{3,2},{4,5},{5,4},{6,7},{7,6},{8,9},{9,8},{10,11... | collective-permute-start | bytes 98312 | tf_op jit(solution)/shard_map/ppermute | solution.py:264
  6.7 0.0 copy-done
  6.7 0.1 pad_add_fusion.where
  7.5 0.1 pad.3.clone
  7.6 0.0 copy-start.1
  7.6 1.0 %copy-done.1 = f32[2,32,32,3,3]{2,1,4,3,0:T(8,128)S(1)} copy-done((f32[2,32,32,3,3]{2,1,4,3,0:T(8,128)S(1)}, f32[2,32,32,3,3]{2,1,4,3,0:T(8,128)}, u32[]{:S(2)}) %copy-start.1) | copy-done | bytes 73752
  8.5 0.0 copy-start.2
  8.5 0.8 %copy-done.2 = f32[1,32,256]{2,1,0:T(8,128)S(1)} copy-done((f32[1,32,256]{2,1,0:T(8,128)S(1)}, f32[1,32,256]{2,1,0:T(8,128)}, u32[]{:S(2)}) %copy-start.2) | copy-done | bytes 32792
  9.3 0.0 copy-start.3
  9.3 0.7 %copy-done.3 = f32[3,32]{1,0:T(4,128)S(1)} copy-done((f32[3,32]{1,0:T(4,128)S(1)}, f32[3,32]{1,0:T(4,128)}, u32[]{:S(2)}) %copy-start.3) | copy-done | bytes 408
  10.0 0.7 %prepare.1 = (bf16[256,144]{1,0:T(8,128)(2,1)S(1)}, bf16[2,576,256]{2,1,0:T(8,128)(2,1)S(1)}, bf16[2,576,256]{2,1,0:T(8,128)(2,1)S(1)}, f32[3,32,256]{2,1,0:T(8,128)S(1)}, f32[32,256]{1,0:T(8,128)S(1)}) custom-call(f32[2,3,3,32,32]{4,3,2,1,0:T(8,128)S(1)} %bitcast.8, f32[9,32]{1,0:T(8,128)S(1)} %reshape.7.first_ref, f32[3,32]{1,0:T(4,128)S(1)} %copy-done.3, ...), custom_call_target="tpu_custom_call" | custom-call | flops 1000000 | bytes 3000000 | tf_op jit(solution)/shard_map/prepare/pallas_call | solution.py:266
  10.7 0.0 collective-permute-done.1
  10.7 0.0 collective-permute-done
  10.7 0.1 maximum_maximum_fusion.image_ref.own_ref
  10.8 0.7 %collective-permute-start.3 = (f32[64,256]{1,0:T(8,128)S(1)}, f32[64,256]{1,0:T(8,128)S(1)}, u32[]{:S(2)}, u32[]{:S(2)}) collective-permute-start(f32[64,256]{1,0:T(8,128)S(1)} %maximum_maximum_fusion.image_ref.own_ref), channel_id=1, source_target_pairs={{4,8},{8,4},{5,9},{9,5},{6,10},{10,6},{7,11},{11,7},{20,24},{24,20... | collective-permute-start | bytes 196616 | tf_op jit(solution)/shard_map/ppermute | solution.py:279
  11.4 2.9 %collective-permute-start.2 = (f32[64,256]{1,0:T(8,128)S(1)}, f32[64,256]{1,0:T(8,128)S(1)}, u32[]{:S(2)}, u32[]{:S(2)}) collective-permute-start(f32[64,256]{1,0:T(8,128)S(1)} %maximum_maximum_fusion.image_ref.own_ref), channel_id=1, source_target_pairs={{0,4},{4,0},{8,12},{12,8},{1,5},{5,1},{9,13},{13,9},{2,6},{6,2},{1... | collective-permute-start | bytes 196616 | tf_op jit(solution)/shard_map/ppermute | solution.py:278
  14.4 0.0 copy-start.4
  14.4 5.0 %own_features.1.packed = bf16[4,2,1152,256]{3,2,1,0:T(8,128)(2,1)S(1)} custom-call(s32[3]{0:T(128)S(1)} %pad_add_fusion.where, f32[64,256]{1,0:T(8,128)S(1)} %maximum_maximum_fusion.image_ref.own_ref, bf16[256,144]{1,0:T(8,128)(2,1)S(1)} %get-tuple-element.11.t1, bf16[2,576,256]{2,1,0:T(8,128)(2,1)S(1)} %get-tuple-element.12.t2, ...), custom_call_target="tpu_custom_call" | custom-call | flops 5000000000 | bytes 10000000 | tf_op jit(solution)/shard_map/own_features/pallas_call | solution.py:281
  19.4 0.0 collective-permute-done.3.odd_ref
  19.4 0.0 collective-permute-done.2.even_ref
  19.4 0.0 copy-done.4
  19.4 10.2 %correlate.1 = f32[8,289]{1,0:T(8,128)} custom-call(s32[3]{0:T(128)S(1)} %pad_add_fusion.where, s32[1]{0:T(128)S(6)} %copy.8.pair, s32[8]{0:T(128)S(1)} %bitcast.12, f32[64,256]{1,0:T(8,128)S(1)} %maximum_maximum_fusion.image_ref.own_ref, f32[64,256]{1,0:T(8,128)S(1)} %collective-permute-done.2.even_ref, f32[64,256]{1,0:T(8,128)S(1)} %collective-permute-done.3.odd_ref, ...), custom_call_target="tpu_custom_call" | custom-call | flops 10000000000 | bytes 10000000 | tf_op jit(solution)/shard_map/correlate/pallas_call | solution.py:288
  (4 shorter events, 0.0 us)
Async XLA Ops:
  0.0 6.7 %copy-start = (f32[32,1,3,3]{0,1,3,2:T(1,128)S(1)}, f32[32,1,3,3]{0,1,3,2:T(1,128)}, u32[]{:S(2)}) copy-start(f32[32,1,3,3]{0,1,3,2:T(1,128)} %param.9) | copy-start | bytes 3460
  0.0 10.7 %collective-permute-start.1 = (f32[32,256]{1,0:T(8,128)}, f32[32,256]{1,0:T(8,128)S(1)}, u32[]{:S(2)}, u32[]{:S(2)}) collective-permute-start(f32[32,256]{1,0:T(8,128)} %bitcast.9), channel_id=1, source_target_pairs={{1,2},{2,1},{5,6},{6,5},{9,10},{10,9},{13,14},{14,13},{17,18},{18,... | collective-permute-start | bytes 98312 | tf_op jit(solution)/shard_map/ppermute | solution.py:265
  0.8 9.9 %collective-permute-start = (f32[32,256]{1,0:T(8,128)}, f32[32,256]{1,0:T(8,128)S(1)}, u32[]{:S(2)}, u32[]{:S(2)}) collective-permute-start(f32[32,256]{1,0:T(8,128)} %bitcast.10), channel_id=1, source_target_pairs={{0,1},{1,0},{2,3},{3,2},{4,5},{5,4},{6,7},{7,6},{8,9},{9,8},{10,11... | collective-permute-start | bytes 98312 | tf_op jit(solution)/shard_map/ppermute | solution.py:264
  7.6 1.0 %copy-start.1 = (f32[2,32,32,3,3]{2,1,4,3,0:T(8,128)S(1)}, f32[2,32,32,3,3]{2,1,4,3,0:T(8,128)}, u32[]{:S(2)}) copy-start(f32[2,32,32,3,3]{2,1,4,3,0:T(8,128)} %param.10) | copy-start | bytes 221188
  8.5 0.8 %copy-start.2 = (f32[1,32,256]{2,1,0:T(8,128)S(1)}, f32[1,32,256]{2,1,0:T(8,128)}, u32[]{:S(2)}) copy-start(f32[1,32,256]{2,1,0:T(8,128)} %param.6) | copy-start | bytes 98308
  9.3 0.7 %copy-start.3 = (f32[3,32]{1,0:T(4,128)S(1)}, f32[3,32]{1,0:T(4,128)}, u32[]{:S(2)}) copy-start(f32[3,32]{1,0:T(4,128)} %bias_ref.1) | copy-start | bytes 1156
  10.8 8.6 %collective-permute-start.3 = (f32[64,256]{1,0:T(8,128)S(1)}, f32[64,256]{1,0:T(8,128)S(1)}, u32[]{:S(2)}, u32[]{:S(2)}) collective-permute-start(f32[64,256]{1,0:T(8,128)S(1)} %maximum_maximum_fusion.image_ref.own_ref), channel_id=1, source_target_pairs={{4,8},{8,4},{5,9},{9,5},{6,10},{10,6},{7,11},{11,7},{20,24},{24,20... | collective-permute-start | bytes 196616 | tf_op jit(solution)/shard_map/ppermute | solution.py:279
  11.4 7.9 %collective-permute-start.2 = (f32[64,256]{1,0:T(8,128)S(1)}, f32[64,256]{1,0:T(8,128)S(1)}, u32[]{:S(2)}, u32[]{:S(2)}) collective-permute-start(f32[64,256]{1,0:T(8,128)S(1)} %maximum_maximum_fusion.image_ref.own_ref), channel_id=1, source_target_pairs={{0,4},{4,0},{8,12},{12,8},{1,5},{5,1},{9,13},{13,9},{2,6},{6,2},{1... | collective-permute-start | bytes 196616 | tf_op jit(solution)/shard_map/ppermute | solution.py:278
  14.4 5.0 %copy-start.4 = (s32[1,1,8]{2,1,0:T(1,128)S(1)}, s32[1,1,8]{2,1,0:T(1,128)}, u32[]{:S(2)}) copy-start(s32[1,1,8]{2,1,0:T(1,128)} %param.8) | copy-start | bytes 100

commit v3 on v2

--- a/solution.py
+++ b/solution.py
@@ -47,8 +47,17 @@
     return lax.broadcasted_iota(jnp.int32, shape, axis)
 
 
-def prepare(later_ref, first_ref, bias_ref, image_ref, t1, t2, t3, spread, image):
-    image[...] = image_ref[...]
+def prepare(later_hbm, first_hbm, bias_hbm, image_hbm, t1, t2, t3, spread, image,
+            later_ref, first_ref, bias_ref, arrived):
+    copies = [
+        pltpu.make_async_copy(source, target, arrived.at[i])
+        for i, (source, target) in enumerate((
+            (later_hbm, later_ref), (first_hbm, first_ref), (bias_hbm, bias_ref), (image_hbm, image)))
+    ]
+    for copy in copies:
+        copy.start()
+    for copy in copies:
+        copy.wait()
     for layer, t in enumerate((t2, t3)):
         for kx in range(3):
             taps = [later_ref[layer, ky, kx] for ky in range(3)]
@@ -56,17 +65,15 @@
             wide = jnp.concatenate([wide, jnp.zeros((C, LANES), f32)], axis=1)
             for yo in range(GROUP):
                 high, low = split(pltpu.roll(wide, yo * C, 1) if yo else wide)
-                rows = slice((kx * GROUP + yo) * C, (kx * GROUP + yo + 1) * C)
+                rows = slice((yo * 3 + kx) * C, (yo * 3 + kx + 1) * C)
                 t[0, rows, :] = high
                 t[1, rows, :] = low
-    taps = first_ref[...]
-    taps = jnp.concatenate([taps] * (WIDTH // C), axis=1)
     offset = iota((16, WIDTH), 0) - iota((16, WIDTH), 1) // C
     pieces = []
     for kx in range(3):
         piece = jnp.zeros((16, WIDTH), f32)
         for ky in range(3):
-            row = taps[3 * ky + kx:3 * ky + kx + 1, :]
+            row = jnp.concatenate([first_ref[ky, kx]] * (WIDTH // C), axis=1)
             piece = jnp.where(offset == ky, jnp.broadcast_to(row, (16, WIDTH)), piece)
         pieces.append(piece)
     pieces.append(jnp.zeros((LANES - 48, WIDTH), f32))
@@ -106,11 +113,8 @@
         rows = slice(group * GROUP * C, (group * GROUP + 8) * C)
         th, tl, xh, xl = t[0], t[1], x[0, rows, :], x[1, rows, :]
         r = dot(jnp.concatenate([th, tl, th], 1), jnp.concatenate([xh, xh, xl], 0))
-        n = GROUP * C
         for yo in range(GROUP):
-            a = r[yo * C:(yo + 1) * C]
-            b = r[n + yo * C:n + (yo + 1) * C]
-            c = r[2 * n + yo * C:2 * n + (yo + 1) * C]
+            a, b, c = (r[(yo * 3 + kx) * C:(yo * 3 + kx + 1) * C] for kx in range(3))
             a = jnp.where(edge == 0, 0.0, pltpu.roll(a, 1, 1))
             c = jnp.where(edge == WIDTH - 1, 0.0, pltpu.roll(c, WIDTH - 1, 1))
             yield group * GROUP + yo, a + b + c + bias
@@ -237,12 +241,13 @@
 
 
 VMEM = pl.BlockSpec(memory_space=pltpu.VMEM)
+HBM = pl.BlockSpec(memory_space=pltpu.HBM)
 SMEM = pl.BlockSpec(memory_space=pltpu.SMEM)
 
 
-def params(flops, moved):
+def params(flops, moved, mib=40):
     return dict(
-        compiler_params=pltpu.CompilerParams(vmem_limit_bytes=40 << 20),
+        compiler_params=pltpu.CompilerParams(vmem_limit_bytes=mib << 20),
         cost_estimate=pl.CostEstimate(flops=flops, bytes_accessed=moved, transcendentals=0),
     )
 
@@ -267,9 +272,12 @@
         prepare,
         out_shape=[shape((256, 144), bf16), shape((2, 576, 256), bf16), shape((2, 576, 256), bf16),
                    shape((LAYERS, C, WIDTH), f32), shape(image.shape, f32)],
-        in_specs=[VMEM] * 4, out_specs=[VMEM] * 5, name="prepare", **params(10**6, 3 * 10**6),
-    )(jnp.transpose(later_kernels, (0, 3, 4, 1, 2)),
-      jnp.transpose(first_kernel, (2, 3, 1, 0)).reshape(9, C), biases, image)
+        in_specs=[HBM] * 4, out_specs=[VMEM] * 5,
+        scratch_shapes=[pltpu.VMEM((2, 3, 3, C, C), f32), pltpu.VMEM((3, 3, 1, C), f32),
+                        pltpu.VMEM((LAYERS, C), f32), pltpu.SemaphoreType.DMA((4,))],
+        name="prepare", **params(10**6, 3 * 10**6),
+    )(*(pltpu.with_memory_space_constraint(v, pltpu.HBM) for v in (
+        jnp.transpose(later_kernels, (0, 3, 4, 1, 2)), jnp.transpose(first_kernel, (2, 3, 1, 0)), biases, image)))
 
     odd_tile = (tile % 2) == 1
     above = jnp.where(odd_tile, got_even[rows - HALO:], got_odd[rows - HALO:])

time: 29.9 us -> 28 us (0.936)
  local copies, waits for them, and re-layouts: 2.52 us -> 0.08 us
  Pallas kernels: 15.9 us -> 16.7 us
    unnamed x10 -> x2, local copies, waits for them, and re-layouts: 2.41 us -> 0.01 us
    pallas_call x1, Pallas kernels: 0.7 us -> 1.72 us  [body(): pl.pallas_call(prepare, out_shape=[shape((256, 144), bf16), shape((2, 576...]
  transfers between devices with their start and end apart: 4 -> 4, of which waited for: 0 -> 0; matrix products, arithmetic and copies ran while one was open for 1% -> 1% of each run, Pallas kernels for 19% -> 24%
where the time goes in v3:
time: 28 us; the launch traced here: 27.8 us
  Pallas kernels  16.7 us (60%)
  starting transfers between devices  10.1 us (36%)
  between operations  0.74 us (3%)
    pallas_call x1, Pallas kernels, body(): pl.pallas_call(correlate, out_shape=shape((8, SHIFTS * SHIFTS), f32), in_...  10.1 us
    ppermute x1, starting transfers between devices, body(): got_even = lax.ppermute(image, 'tile', pairs_even(tiles))  5.91 us
    pallas_call x1, Pallas kernels, body(): pl.pallas_call(own_features, out_shape=shape((WIDTH // WIN, 2, DEEP, WIDT...  4.9 us
    ppermute x1, starting transfers between devices, body(): even = lax.ppermute(own, 'sec', pairs_even(sections))  2.92 us
    pallas_call x1, Pallas kernels, body(): pl.pallas_call(prepare, out_shape=[shape((256, 144), bf16), shape((2, 576...  1.72 us
    ppermute x1, starting transfers between devices, body(): odd = lax.ppermute(own, 'sec', pairs_odd(sections))  0.65 us
    ppermute x1, starting transfers between devices, body(): got_odd = lax.ppermute(image, 'tile', pairs_odd(tiles))  0.65 us
  transfers between devices with their start and end apart: 4, of which 0 were waited for; matrix products, arithmetic and copies ran while one was open for 1% of the time, Pallas kernels for 24%

profile of v3, /device:TPU:0, one launch (start us, length us, event | category | flops | bytes accessed | tf_op | source)
XLA Modules:
  0.0 27.8 jit_solution(3314468125770300566)
XLA Ops:
  0.0 0.7 %collective-permute-start.1 = (f32[32,256]{1,0:T(8,128)}, f32[32,256]{1,0:T(8,128)S(1)}, u32[]{:S(2)}, u32[]{:S(2)}) collective-permute-start(f32[32,256]{1,0:T(8,128)} %bitcast.9), channel_id=1, source_target_pairs={{1,2},{2,1},{5,6},{6,5},{9,10},{10,9},{13,14},{14,13},{17,18},{18,... | collective-permute-start | bytes 98312 | tf_op jit(solution)/shard_map/ppermute | solution.py:270
  0.7 5.9 %collective-permute-start = (f32[32,256]{1,0:T(8,128)}, f32[32,256]{1,0:T(8,128)S(1)}, u32[]{:S(2)}, u32[]{:S(2)}) collective-permute-start(f32[32,256]{1,0:T(8,128)} %bitcast.10), channel_id=1, source_target_pairs={{0,1},{1,0},{2,3},{3,2},{4,5},{5,4},{6,7},{7,6},{8,9},{9,8},{10,11... | collective-permute-start | bytes 98312 | tf_op jit(solution)/shard_map/ppermute | solution.py:269
  6.6 0.1 pad_add_fusion.where
  7.3 0.1 pad.3.clone
  7.4 1.7 %prepare.1 = (bf16[256,144]{1,0:T(8,128)(2,1)S(1)}, bf16[2,576,256]{2,1,0:T(8,128)(2,1)S(1)}, bf16[2,576,256]{2,1,0:T(8,128)(2,1)S(1)}, f32[3,32,256]{2,1,0:T(8,128)S(1)}, f32[32,256]{1,0:T(8,128)S(1)}) custom-call(f32[2,3,3,32,32]{4,3,2,1,0:T(8,128)} %bitcast.8, f32[3,3,1,32]{3,2,1,0:T(1,128)} %bitcast.12, f32[3,32]{1,0:T(4,128)} %bias_hbm.1, ...), custom_call_target="tpu_custom_call" | custom-call | flops 1000000 | bytes 3000000 | tf_op jit(solution)/shard_map/prepare/pallas_call | solution.py:271
  9.1 0.0 collective-permute-done.1
  9.1 0.0 collective-permute-done
  9.2 0.1 maximum_maximum_fusion.image_ref.own_ref
  9.2 0.7 %collective-permute-start.3 = (f32[64,256]{1,0:T(8,128)S(1)}, f32[64,256]{1,0:T(8,128)S(1)}, u32[]{:S(2)}, u32[]{:S(2)}) collective-permute-start(f32[64,256]{1,0:T(8,128)S(1)} %maximum_maximum_fusion.image_ref.own_ref), channel_id=1, source_target_pairs={{4,8},{8,4},{5,9},{9,5},{6,10},{10,6},{7,11},{11,7},{20,24},{24,20... | collective-permute-start | bytes 196616 | tf_op jit(solution)/shard_map/ppermute | solution.py:287
  9.9 2.9 %collective-permute-start.2 = (f32[64,256]{1,0:T(8,128)S(1)}, f32[64,256]{1,0:T(8,128)S(1)}, u32[]{:S(2)}, u32[]{:S(2)}) collective-permute-start(f32[64,256]{1,0:T(8,128)S(1)} %maximum_maximum_fusion.image_ref.own_ref), channel_id=1, source_target_pairs={{0,4},{4,0},{8,12},{12,8},{1,5},{5,1},{9,13},{13,9},{2,6},{6,2},{1... | collective-permute-start | bytes 196616 | tf_op jit(solution)/shard_map/ppermute | solution.py:286
  12.8 0.0 copy-start
  12.8 4.9 %own_features.1.packed = bf16[4,2,1152,256]{3,2,1,0:T(8,128)(2,1)S(1)} custom-call(s32[3]{0:T(128)S(1)} %pad_add_fusion.where, f32[64,256]{1,0:T(8,128)S(1)} %maximum_maximum_fusion.image_ref.own_ref, bf16[256,144]{1,0:T(8,128)(2,1)S(1)} %get-tuple-element.11.t1, bf16[2,576,256]{2,1,0:T(8,128)(2,1)S(1)} %get-tuple-element.12.t2, ...), custom_call_target="tpu_custom_call" | custom-call | flops 5000000000 | bytes 10000000 | tf_op jit(solution)/shard_map/own_features/pallas_call | solution.py:289
  17.7 0.0 collective-permute-done.3.odd_ref
  17.7 0.0 collective-permute-done.2.even_ref
  17.7 0.0 copy-done
  17.7 10.1 %correlate.1 = f32[8,289]{1,0:T(8,128)} custom-call(s32[3]{0:T(128)S(1)} %pad_add_fusion.where, s32[1]{0:T(128)S(6)} %copy.7.pair, s32[8]{0:T(128)S(1)} %bitcast.7, f32[64,256]{1,0:T(8,128)S(1)} %maximum_maximum_fusion.image_ref.own_ref, f32[64,256]{1,0:T(8,128)S(1)} %collective-permute-done.2.even_ref, f32[64,256]{1,0:T(8,128)S(1)} %collective-permute-done.3.odd_ref, ...), custom_call_target="tpu_custom_call" | custom-call | flops 10000000000 | bytes 10000000 | tf_op jit(solution)/shard_map/correlate/pallas_call | solution.py:296
  (2 shorter events, 0.0 us)
Async XLA Ops:
  0.0 9.1 %collective-permute-start.1 = (f32[32,256]{1,0:T(8,128)}, f32[32,256]{1,0:T(8,128)S(1)}, u32[]{:S(2)}, u32[]{:S(2)}) collective-permute-start(f32[32,256]{1,0:T(8,128)} %bitcast.9), channel_id=1, source_target_pairs={{1,2},{2,1},{5,6},{6,5},{9,10},{10,9},{13,14},{14,13},{17,18},{18,... | collective-permute-start | bytes 98312 | tf_op jit(solution)/shard_map/ppermute | solution.py:270
  0.7 8.5 %collective-permute-start = (f32[32,256]{1,0:T(8,128)}, f32[32,256]{1,0:T(8,128)S(1)}, u32[]{:S(2)}, u32[]{:S(2)}) collective-permute-start(f32[32,256]{1,0:T(8,128)} %bitcast.10), channel_id=1, source_target_pairs={{0,1},{1,0},{2,3},{3,2},{4,5},{5,4},{6,7},{7,6},{8,9},{9,8},{10,11... | collective-permute-start | bytes 98312 | tf_op jit(solution)/shard_map/ppermute | solution.py:269
  9.2 8.5 %collective-permute-start.3 = (f32[64,256]{1,0:T(8,128)S(1)}, f32[64,256]{1,0:T(8,128)S(1)}, u32[]{:S(2)}, u32[]{:S(2)}) collective-permute-start(f32[64,256]{1,0:T(8,128)S(1)} %maximum_maximum_fusion.image_ref.own_ref), channel_id=1, source_target_pairs={{4,8},{8,4},{5,9},{9,5},{6,10},{10,6},{7,11},{11,7},{20,24},{24,20... | collective-permute-start | bytes 196616 | tf_op jit(solution)/shard_map/ppermute | solution.py:287
  9.9 7.8 %collective-permute-start.2 = (f32[64,256]{1,0:T(8,128)S(1)}, f32[64,256]{1,0:T(8,128)S(1)}, u32[]{:S(2)}, u32[]{:S(2)}) collective-permute-start(f32[64,256]{1,0:T(8,128)S(1)} %maximum_maximum_fusion.image_ref.own_ref), channel_id=1, source_target_pairs={{0,4},{4,0},{8,12},{12,8},{1,5},{5,1},{9,13},{13,9},{2,6},{6,2},{1... | collective-permute-start | bytes 196616 | tf_op jit(solution)/shard_map/ppermute | solution.py:286
  12.8 4.9 %copy-start = (s32[1,1,8]{2,1,0:T(1,128)S(1)}, s32[1,1,8]{2,1,0:T(1,128)}, u32[]{:S(2)}) copy-start(s32[1,1,8]{2,1,0:T(1,128)} %param.8) | copy-start | bytes 100

commit v4 on v3

--- a/solution.py
+++ b/solution.py
@@ -13,7 +13,6 @@
 SHIFTS = 2 * RADIUS + 1
 HALO = RADIUS + LAYERS
 RAW_ROWS = 64
-GROUP = 6
 LANES = 128
 WIDTH = 256
 WIN = 64
@@ -22,6 +21,8 @@
 STEPS = 5
 DEEP = (BLK + JOINT) * C
 BAND = 24
+STREAMS = ((1, 2), (None, 0), (0, 1), (2, None))
+FORMS = ((1, 0), (2, 1), (0, None), (None, 2))
 bf16 = jnp.bfloat16
 f32 = jnp.float32
 
@@ -47,7 +48,7 @@
     return lax.broadcasted_iota(jnp.int32, shape, axis)
 
 
-def prepare(later_hbm, first_hbm, bias_hbm, image_hbm, t1, t2, t3, spread, image,
+def prepare(later_hbm, first_hbm, bias_hbm, image_hbm, t1, t2, t3, spread, order, image,
             later_ref, first_ref, bias_ref, arrived):
     copies = [
         pltpu.make_async_copy(source, target, arrived.at[i])
@@ -56,103 +57,125 @@
     ]
     for copy in copies:
         copy.start()
+    row, col = iota((WIDTH, WIDTH), 0), iota((WIDTH, WIDTH), 1)
+    order[0:WIDTH, :] = jnp.where(row == 2 * (col % LANES) + col // LANES, 1.0, 0.0).astype(bf16)
+    order[WIDTH:, :] = jnp.where(col == 2 * (row % LANES) + row // LANES, 1.0, 0.0).astype(bf16)
     for copy in copies:
         copy.wait()
+    nothing = jnp.zeros((C, C), f32)
     for layer, t in enumerate((t2, t3)):
-        for kx in range(3):
-            taps = [later_ref[layer, ky, kx] for ky in range(3)]
-            wide = jnp.concatenate(taps + [jnp.zeros((C, LANES - 3 * C), f32)], axis=1)
-            wide = jnp.concatenate([wide, jnp.zeros((C, LANES), f32)], axis=1)
-            for yo in range(GROUP):
-                high, low = split(pltpu.roll(wide, yo * C, 1) if yo else wide)
-                rows = slice((yo * 3 + kx) * C, (yo * 3 + kx + 1) * C)
+        for stream, (even, odd) in enumerate(STREAMS):
+            taps = []
+            for ky in range(3):
+                taps += [nothing if kx is None else later_ref[layer, ky, kx] for kx in (even, odd)]
+            wide = jnp.concatenate(taps + [nothing, nothing], axis=1)
+            for yo in range(2):
+                high, low = split(pltpu.roll(wide, yo * 2 * C, 1) if yo else wide)
+                rows = slice((yo * 4 + stream) * C, (yo * 4 + stream + 1) * C)
                 t[0, rows, :] = high
                 t[1, rows, :] = low
-    offset = iota((16, WIDTH), 0) - iota((16, WIDTH), 1) // C
+    shape = (16, 8 * 2 * C)
+    offset = iota(shape, 0) - iota(shape, 1) // (2 * C)
     pieces = []
-    for kx in range(3):
-        piece = jnp.zeros((16, WIDTH), f32)
+    for even, odd in FORMS:
+        piece = jnp.zeros(shape, f32)
         for ky in range(3):
-            row = jnp.concatenate([first_ref[ky, kx]] * (WIDTH // C), axis=1)
-            piece = jnp.where(offset == ky, jnp.broadcast_to(row, (16, WIDTH)), piece)
+            pair = [jnp.zeros((1, C), f32) if kx is None else first_ref[ky, kx] for kx in (even, odd)]
+            piece = jnp.where(offset == ky, jnp.broadcast_to(jnp.concatenate(pair * 8, 1), shape), piece)
         pieces.append(piece)
-    pieces.append(jnp.zeros((LANES - 48, WIDTH), f32))
+    pieces.append(jnp.zeros((64, 8 * 2 * C), f32))
     high, low = split(jnp.transpose(jnp.concatenate(pieces, 0)))
-    t1[:, 0:48] = high[:, 0:48]
-    t1[:, 48:96] = low[:, 0:48]
-    t1[:, 96:144] = high[:, 0:48]
+    t1[:, 0:64] = high[:, 0:64]
+    t1[:, 64:128] = low[:, 0:64]
+    t1[:, 128:192] = high[:, 0:64]
     b = jnp.concatenate([bias_ref[...], jnp.zeros((LAYERS, LANES - C), f32)], 1)
     b = jnp.transpose(jnp.concatenate([b, jnp.zeros((8 - LAYERS, LANES), f32)], 0))
     for layer in range(LAYERS):
         spread[layer] = jnp.broadcast_to(b[0:C, layer:layer + 1], (C, WIDTH))
 
 
-def encode(image, base, groups, ends, tile, tiles, t1, t2, t3, spread, raw, x1, x2, emit):
-    n1, n2 = 8 * groups[0], GROUP * groups[1]
-    col = iota((RAW_ROWS, WIDTH), 1)
-    raw[0] = jnp.where(col == 0, 0.0, pltpu.roll(image, 1, 1))
-    raw[1] = image
-    raw[2] = jnp.where(col == WIDTH - 1, 0.0, pltpu.roll(image, WIDTH - 1, 1))
-    edge = iota((C, WIDTH), 1)
+def encode(image, starts, groups, ends, tile, tiles, t1, t2, t3, spread, order, raw, x1, x2, x3, emit):
+    n1, n2, n3 = 8 * groups[0], 2 * groups[1], 2 * groups[2]
+    h = image.astype(bf16)
+    rest = image - h.astype(f32)
+    m = rest.astype(bf16)
+    l = (rest - m.astype(f32)).astype(bf16)
+    apart = order[0:WIDTH, :]
+    image = dot(jnp.concatenate([h, m, l], 1), jnp.concatenate([apart] * 3, 0))
+    even, odd = image[:, :LANES], image[:, LANES:]
+    col = iota((RAW_ROWS, LANES), 1)
+    before = jnp.where(col == 0, 0.0, pltpu.roll(odd, 1, 1))
+    after = jnp.where(col == LANES - 1, 0.0, pltpu.roll(even, LANES - 1, 1))
+    for form, v in enumerate((even, odd, before, after)):
+        raw[form] = jnp.concatenate([v[a:a + n1 + 8] for a in starts], 1)
+    lane = iota((C, WIDTH), 1) % LANES
+    twice = lambda v: jnp.concatenate([v, v], 0)
 
     def put(x, row, value):
         high, low = split(value)
-        x[0, row * C:(row + 1) * C, :] = high
-        x[1, row * C:(row + 1) * C, :] = low
+        x[0, row * 2 * C:(row + 1) * 2 * C, :] = high
+        x[1, row * 2 * C:(row + 1) * 2 * C, :] = low
 
     def outside(x, top, end, rows):
         @pl.when(tile == 0)
         def _():
-            x[:, 0:top * C, :] = jnp.zeros((2, top * C, WIDTH), bf16)
+            x[:, 0:top * 2 * C, 0:LANES] = jnp.zeros((2, top * 2 * C, LANES), bf16)
 
         @pl.when(tile == tiles - 1)
         def _():
-            x[:, end * C:rows * C, :] = jnp.zeros((2, (rows - end) * C, WIDTH), bf16)
-
-    def conv(t, x, group, bias):
-        rows = slice(group * GROUP * C, (group * GROUP + 8) * C)
+            x[:, end * 2 * C:rows * 2 * C, LANES:] = jnp.zeros((2, (rows - end) * 2 * C, LANES), bf16)
+
+    def shifted(v, by, blank):
+        v = jnp.concatenate([pltpu.roll(v[:, i:i + LANES], by, 1) for i in range(0, WIDTH, LANES)], 1)
+        return jnp.where(lane == blank, 0.0, v)
+
+    def conv(t, x, step, bias):
+        rows = slice(step * 4 * C, (step * 4 + 8) * C)
         th, tl, xh, xl = t[0], t[1], x[0, rows, :], x[1, rows, :]
         r = dot(jnp.concatenate([th, tl, th], 1), jnp.concatenate([xh, xh, xl], 0))
-        for yo in range(GROUP):
-            a, b, c = (r[(yo * 3 + kx) * C:(yo * 3 + kx + 1) * C] for kx in range(3))
-            a = jnp.where(edge == 0, 0.0, pltpu.roll(a, 1, 1))
-            c = jnp.where(edge == WIDTH - 1, 0.0, pltpu.roll(c, WIDTH - 1, 1))
-            yield group * GROUP + yo, a + b + c + bias
+        for yo in range(2):
+            a, b, c, d = (r[(yo * 4 + i) * C:(yo * 4 + i + 1) * C] for i in range(4))
+            yield 2 * step + yo, a + shifted(b, 1, 0) + bias, c + shifted(d, LANES - 1, LANES - 1) + bias
 
     for g in range(groups[0]):
-        parts = [raw[kx, base + 8 * g:base + 8 * g + 16, :] for kx in range(3)]
-        high, low = split(jnp.concatenate(parts, 0))
+        high, low = split(jnp.concatenate([raw[form, 8 * g:8 * g + 16, :] for form in range(4)], 0))
         r = dot(t1[...], jnp.concatenate([high, high, low], 0))
         for yo in range(8):
-            put(x1, 8 * g + yo, jnp.tanh(r[yo * C:(yo + 1) * C] + spread[0]))
+            put(x1, 8 * g + yo, jnp.tanh(r[yo * 2 * C:(yo + 1) * 2 * C] + twice(spread[0])))
     outside(x1, ends[0], ends[1], n1)
-    for g in range(groups[1]):
-        for row, value in conv(t2, x1, g, spread[1]):
-            put(x2, row, jnp.tanh(value))
+    for step in range(groups[1]):
+        for row, a, b in conv(t2, x1, step, spread[1]):
+            put(x2, row, jnp.tanh(jnp.concatenate([a, b], 0)))
     outside(x2, ends[2], ends[3], n2)
-    for row in range(n2, GROUP * groups[2] + 2):
-        x2[:, row * C:(row + 1) * C, :] = jnp.zeros((2, C, WIDTH), bf16)
-    for g in range(groups[2]):
-        for row, value in conv(t3, x2, g, spread[2]):
-            emit(row, value)
-
-
-def own_features(where, image_ref, t1, t2, t3, spread, packed, raw, x1, x2, kept):
+    for step in range(groups[2]):
+        for row, a, b in conv(t3, x2, step, spread[2]):
+            for run in range(2):
+                rows = slice((run * n3 + row) * C, (run * n3 + row + 1) * C)
+                for parity, v in enumerate((a, b)):
+                    high, low = split(v[:, run * LANES:(run + 1) * LANES])
+                    x3[rows, parity * LANES:(parity + 1) * LANES] = high
+                    x3[rows, WIDTH + parity * LANES:WIDTH + (parity + 1) * LANES] = low
+    together = jnp.concatenate([order[WIDTH:, :]] * 2, 0)
+    for row in range(0, 2 * n3, 16):
+        r = dot(x3[row * C:(row + 16) * C, :], together)
+        for i in range(16):
+            emit(row + i, r[i * C:(i + 1) * C])
+
+
+def own_features(where, image_ref, t1, t2, t3, spread, order, packed, raw, x1, x2, x3, kept):
     tile, tiles = where[0], where[1]
     pad = JOINT - 1
     kept[:, :, 0:pad * C, :] = jnp.zeros((2, 2, pad * C, WIDTH), bf16)
     kept[:, :, (pad + BLK) * C:, :] = jnp.zeros((2, 2, JOINT * C, WIDTH), bf16)
 
     def emit(row, value):
-        if row >= BLK:
-            return
         turned = [pltpu.roll(value[:, i:i + LANES], WIN, 1) for i in range(0, WIDTH, LANES)]
         rows = slice((row + pad) * C, (row + pad + 1) * C)
         for form, v in enumerate((value, jnp.concatenate(turned, 1))):
             kept[form, 0, rows, :], kept[form, 1, rows, :] = split(v)
 
-    encode(image_ref[...], RADIUS, (5, 6, 6), (2, 34, 1, 33), tile, tiles,
-           t1, t2, t3, spread, raw, x1, x2, emit)
+    encode(image_ref[...], (8, 24), (3, 9, 8), (2, 18, 1, 17), tile, tiles,
+           t1, t2, t3, spread, order, raw, x1, x2, x3, emit)
     left = iota((C, LANES), 1) < WIN
     for w in range(WIDTH // WIN):
         half = slice((w // 2) * LANES, (w // 2 + 1) * LANES)
@@ -166,8 +189,8 @@
                 packed[w, part, y * C:(y + 1) * C, :] = jnp.concatenate(cols, 1)
 
 
-def correlate(where, pair, mask, own_ref, even_ref, odd_ref, t1, t2, t3, spread, packed, out_ref,
-              raw, x1, x2, feats, turned):
+def correlate(where, pair, mask, own_ref, even_ref, odd_ref, t1, t2, t3, spread, order, packed, out_ref,
+              raw, x1, x2, x3, feats, turned):
     tile, tiles, section = where[0], where[1], where[2]
     image = jnp.where(pair[0] == section, own_ref[...],
                       jnp.where(pair[0] == (section ^ 1), even_ref[...], odd_ref[...]))
@@ -175,7 +198,8 @@
     def emit(row, value):
         feats[row * C:(row + 1) * C, :] = value
 
-    encode(image, 0, (7, 9, 8), (10, 42, 9, 41), tile, tiles, t1, t2, t3, spread, raw, x1, x2, emit)
+    encode(image, (0, 24), (4, 13, 12), (10, 18, 9, 17), tile, tiles,
+           t1, t2, t3, spread, order, raw, x1, x2, x3, emit)
 
     @pl.when(tile == 0)
     def _():
@@ -252,11 +276,12 @@
     )
 
 
-def scratch(rows1, rows2):
+def scratch(rows1, rows2, rows3):
     return [
-        pltpu.VMEM((3, RAW_ROWS, WIDTH), f32),
-        pltpu.VMEM((2, rows1 * C, WIDTH), bf16),
-        pltpu.VMEM((2, rows2 * C, WIDTH), bf16),
+        pltpu.VMEM((4, rows1 + 8, WIDTH), f32),
+        pltpu.VMEM((2, rows1 * 2 * C, WIDTH), bf16),
+        pltpu.VMEM((2, rows2 * 2 * C, WIDTH), bf16),
+        pltpu.VMEM((rows3 * C, 2 * WIDTH), bf16),
     ]
 
 
@@ -268,11 +293,11 @@
     shape = jax.ShapeDtypeStruct
     got_even = lax.ppermute(image, "tile", pairs_even(tiles))
     got_odd = lax.ppermute(image, "tile", pairs_odd(tiles))
-    t1, t2, t3, spread, image = pl.pallas_call(
+    t1, t2, t3, spread, order, image = pl.pallas_call(
         prepare,
-        out_shape=[shape((256, 144), bf16), shape((2, 576, 256), bf16), shape((2, 576, 256), bf16),
-                   shape((LAYERS, C, WIDTH), f32), shape(image.shape, f32)],
-        in_specs=[HBM] * 4, out_specs=[VMEM] * 5,
+        out_shape=[shape((512, 192), bf16), shape((2, WIDTH, WIDTH), bf16), shape((2, WIDTH, WIDTH), bf16),
+                   shape((LAYERS, C, WIDTH), f32), shape((2 * WIDTH, WIDTH), bf16), shape(image.shape, f32)],
+        in_specs=[HBM] * 4, out_specs=[VMEM] * 6,
         scratch_shapes=[pltpu.VMEM((2, 3, 3, C, C), f32), pltpu.VMEM((3, 3, 1, C), f32),
                         pltpu.VMEM((LAYERS, C), f32), pltpu.SemaphoreType.DMA((4,))],
         name="prepare", **params(10**6, 3 * 10**6),
@@ -289,20 +314,20 @@
     packed = pl.pallas_call(
         own_features,
         out_shape=shape((WIDTH // WIN, 2, DEEP, WIDTH), bf16),
-        in_specs=[SMEM] + [VMEM] * 5, out_specs=VMEM,
-        scratch_shapes=scratch(40, 38) + [pltpu.VMEM((2, 2, (BLK + 2 * JOINT - 1) * C, WIDTH), bf16)],
+        in_specs=[SMEM] + [VMEM] * 6, out_specs=VMEM,
+        scratch_shapes=scratch(24, 18, 32) + [pltpu.VMEM((2, 2, (BLK + 2 * JOINT - 1) * C, WIDTH), bf16)],
         name="own_features", **params(5 * 10**9, 10**7),
-    )(where, own, t1, t2, t3, spread)
+    )(where, own, t1, t2, t3, spread, order)
     result = pl.pallas_call(
         correlate,
         out_shape=shape((8, SHIFTS * SHIFTS), f32),
-        in_specs=[SMEM] * 3 + [VMEM] * 8, out_specs=VMEM,
-        scratch_shapes=scratch(56, 54) + [
+        in_specs=[SMEM] * 3 + [VMEM] * 9, out_specs=VMEM,
+        scratch_shapes=scratch(32, 26, 48) + [
             pltpu.VMEM(((BLK + 2 * RADIUS) * C, WIDTH), f32),
             pltpu.VMEM((2, WIDTH + 2 * RADIUS, (BLK + 2 * RADIUS + JOINT) * C), bf16),
         ],
         name="correlate", **params(10**10, 10**7),
-    )(where, pairing, valid_mask.reshape(-1), own, even, odd, t1, t2, t3, spread, packed)
+    )(where, pairing, valid_mask.reshape(-1), own, even, odd, t1, t2, t3, spread, order, packed)
     return result[None, None]
 
 

time: 28 us -> 27.4 us (0.979)
  Pallas kernels: 16.7 us -> 16.1 us
    pallas_call x1, Pallas kernels: 10.1 us -> 9.4 us  [body(): pl.pallas_call(correlate, out_shape=shape((8, SHIFTS * SHIFTS), f32), in_...]
  transfers between devices with their start and end apart: 4 -> 4, of which waited for: 0 -> 0; matrix products, arithmetic and copies ran while one was open for 1% -> 1% of each run, Pallas kernels for 24% -> 25%
where the time goes in v4:
time: 27.4 us; the launch traced here: 27.3 us
  Pallas kernels  16.1 us (59%)
  starting transfers between devices  10.1 us (37%)
  between operations  0.74 us (3%)
    pallas_call x1, Pallas kernels, body(): pl.pallas_call(correlate, out_shape=shape((8, SHIFTS * SHIFTS), f32), in_...  9.4 us
    ppermute x1, starting transfers between devices, body(): got_even = lax.ppermute(image, 'tile', pairs_even(tiles))  5.91 us
    pallas_call x1, Pallas kernels, body(): pl.pallas_call(own_features, out_shape=shape((WIDTH // WIN, 2, DEEP, WIDT...  4.86 us
    ppermute x1, starting transfers between devices, body(): even = lax.ppermute(own, 'sec', pairs_even(sections))  2.92 us
    pallas_call x1, Pallas kernels, body(): pl.pallas_call(prepare, out_shape=[shape((512, 192), bf16), shape((2, WID...  1.87 us
    ppermute x1, starting transfers between devices, body(): odd = lax.ppermute(own, 'sec', pairs_odd(sections))  0.65 us
    ppermute x1, starting transfers between devices, body(): got_odd = lax.ppermute(image, 'tile', pairs_odd(tiles))  0.65 us
  transfers between devices with their start and end apart: 4, of which 0 were waited for; matrix products, arithmetic and copies ran while one was open for 1% of the time, Pallas kernels for 25%

profile of v4, /device:TPU:0, one launch (start us, length us, event | category | flops | bytes accessed | tf_op | source)
XLA Modules:
  0.0 27.3 jit_solution(13042204964410046312)
XLA Ops:
  0.0 0.7 %collective-permute-start.1 = (f32[32,256]{1,0:T(8,128)}, f32[32,256]{1,0:T(8,128)S(1)}, u32[]{:S(2)}, u32[]{:S(2)}) collective-permute-start(f32[32,256]{1,0:T(8,128)} %bitcast.9), channel_id=1, source_target_pairs={{1,2},{2,1},{5,6},{6,5},{9,10},{10,9},{13,14},{14,13},{17,18},{18,... | collective-permute-start | bytes 98312 | tf_op jit(solution)/shard_map/ppermute | solution.py:295
  0.7 5.9 %collective-permute-start = (f32[32,256]{1,0:T(8,128)}, f32[32,256]{1,0:T(8,128)S(1)}, u32[]{:S(2)}, u32[]{:S(2)}) collective-permute-start(f32[32,256]{1,0:T(8,128)} %bitcast.10), channel_id=1, source_target_pairs={{0,1},{1,0},{2,3},{3,2},{4,5},{5,4},{6,7},{7,6},{8,9},{9,8},{10,11... | collective-permute-start | bytes 98312 | tf_op jit(solution)/shard_map/ppermute | solution.py:294
  6.6 0.1 pad_add_fusion.where
  7.3 0.1 pad.3.clone
  7.4 1.9 %prepare.1 = (bf16[512,192]{1,0:T(8,128)(2,1)S(1)}, bf16[2,256,256]{2,1,0:T(8,128)(2,1)S(1)}, bf16[2,256,256]{2,1,0:T(8,128)(2,1)S(1)}, f32[3,32,256]{2,1,0:T(8,...) custom-call(f32[2,3,3,32,32]{4,3,2,1,0:T(8,128)} %bitcast.8, f32[3,3,1,32]{3,2,1,0:T(1,128)} %bitcast.12, ...), custom_call_target="tpu_custom_call" | custom-call | flops 1000000 | bytes 3000000 | tf_op jit(solution)/shard_map/prepare/pallas_call | solution.py:296
  9.3 0.0 collective-permute-done.1
  9.3 0.0 collective-permute-done
  9.3 0.1 maximum_maximum_fusion.image_ref.own_ref
  9.4 0.7 %collective-permute-start.3 = (f32[64,256]{1,0:T(8,128)S(1)}, f32[64,256]{1,0:T(8,128)S(1)}, u32[]{:S(2)}, u32[]{:S(2)}) collective-permute-start(f32[64,256]{1,0:T(8,128)S(1)} %maximum_maximum_fusion.image_ref.own_ref), channel_id=1, source_target_pairs={{4,8},{8,4},{5,9},{9,5},{6,10},{10,6},{7,11},{11,7},{20,24},{24,20... | collective-permute-start | bytes 196616 | tf_op jit(solution)/shard_map/ppermute | solution.py:312
  10.0 2.9 %collective-permute-start.2 = (f32[64,256]{1,0:T(8,128)S(1)}, f32[64,256]{1,0:T(8,128)S(1)}, u32[]{:S(2)}, u32[]{:S(2)}) collective-permute-start(f32[64,256]{1,0:T(8,128)S(1)} %maximum_maximum_fusion.image_ref.own_ref), channel_id=1, source_target_pairs={{0,4},{4,0},{8,12},{12,8},{1,5},{5,1},{9,13},{13,9},{2,6},{6,2},{1... | collective-permute-start | bytes 196616 | tf_op jit(solution)/shard_map/ppermute | solution.py:311
  13.0 0.0 copy-start
  13.0 4.9 %own_features.1.packed = bf16[4,2,1152,256]{3,2,1,0:T(8,128)(2,1)S(1)} custom-call(s32[3]{0:T(128)S(1)} %pad_add_fusion.where, f32[64,256]{1,0:T(8,128)S(1)} %maximum_maximum_fusion.image_ref.own_ref, bf16[512,192]{1,0:T(8,128)(2,1)S(1)} %get-tuple-element.12.t1, bf16[2,256,256]{2,1,0:T(8,128)(2,1)S(1)} %get-tuple-element.13.t2, ...), custom_call_target="tpu_custom_call" | custom-call | flops 5000000000 | bytes 10000000 | tf_op jit(solution)/shard_map/own_features/pallas_call | solution.py:314
  17.8 0.0 collective-permute-done.3.odd_ref
  17.8 0.0 collective-permute-done.2.even_ref
  17.8 0.0 copy-done
  17.9 9.4 %correlate.1 = f32[8,289]{1,0:T(8,128)} custom-call(s32[3]{0:T(128)S(1)} %pad_add_fusion.where, s32[1]{0:T(128)S(6)} %copy.7.pair, s32[8]{0:T(128)S(1)} %bitcast.7, f32[64,256]{1,0:T(8,128)S(1)} %maximum_maximum_fusion.image_ref.own_ref, f32[64,256]{1,0:T(8,128)S(1)} %collective-permute-done.2.even_ref, f32[64,256]{1,0:T(8,128)S(1)} %collective-permute-done.3.odd_ref, ...), custom_call_target="tpu_custom_call" | custom-call | flops 10000000000 | bytes 10000000 | tf_op jit(solution)/shard_map/correlate/pallas_call | solution.py:321
  (2 shorter events, 0.0 us)
Async XLA Ops:
  0.0 9.3 %collective-permute-start.1 = (f32[32,256]{1,0:T(8,128)}, f32[32,256]{1,0:T(8,128)S(1)}, u32[]{:S(2)}, u32[]{:S(2)}) collective-permute-start(f32[32,256]{1,0:T(8,128)} %bitcast.9), channel_id=1, source_target_pairs={{1,2},{2,1},{5,6},{6,5},{9,10},{10,9},{13,14},{14,13},{17,18},{18,... | collective-permute-start | bytes 98312 | tf_op jit(solution)/shard_map/ppermute | solution.py:295
  0.7 8.6 %collective-permute-start = (f32[32,256]{1,0:T(8,128)}, f32[32,256]{1,0:T(8,128)S(1)}, u32[]{:S(2)}, u32[]{:S(2)}) collective-permute-start(f32[32,256]{1,0:T(8,128)} %bitcast.10), channel_id=1, source_target_pairs={{0,1},{1,0},{2,3},{3,2},{4,5},{5,4},{6,7},{7,6},{8,9},{9,8},{10,11... | collective-permute-start | bytes 98312 | tf_op jit(solution)/shard_map/ppermute | solution.py:294
  9.4 8.4 %collective-permute-start.3 = (f32[64,256]{1,0:T(8,128)S(1)}, f32[64,256]{1,0:T(8,128)S(1)}, u32[]{:S(2)}, u32[]{:S(2)}) collective-permute-start(f32[64,256]{1,0:T(8,128)S(1)} %maximum_maximum_fusion.image_ref.own_ref), channel_id=1, source_target_pairs={{4,8},{8,4},{5,9},{9,5},{6,10},{10,6},{7,11},{11,7},{20,24},{24,20... | collective-permute-start | bytes 196616 | tf_op jit(solution)/shard_map/ppermute | solution.py:312
  10.0 7.8 %collective-permute-start.2 = (f32[64,256]{1,0:T(8,128)S(1)}, f32[64,256]{1,0:T(8,128)S(1)}, u32[]{:S(2)}, u32[]{:S(2)}) collective-permute-start(f32[64,256]{1,0:T(8,128)S(1)} %maximum_maximum_fusion.image_ref.own_ref), channel_id=1, source_target_pairs={{0,4},{4,0},{8,12},{12,8},{1,5},{5,1},{9,13},{13,9},{2,6},{6,2},{1... | collective-permute-start | bytes 196616 | tf_op jit(solution)/shard_map/ppermute | solution.py:311
  13.0 4.9 %copy-start = (s32[1,1,8]{2,1,0:T(1,128)S(1)}, s32[1,1,8]{2,1,0:T(1,128)}, u32[]{:S(2)}) copy-start(s32[1,1,8]{2,1,0:T(1,128)} %param.8) | copy-start | bytes 100

commit v5 on v4

--- a/solution.py
+++ b/solution.py
@@ -48,12 +48,14 @@
     return lax.broadcasted_iota(jnp.int32, shape, axis)
 
 
-def prepare(later_hbm, first_hbm, bias_hbm, image_hbm, t1, t2, t3, spread, order, image,
-            later_ref, first_ref, bias_ref, arrived):
+def prepare(later_hbm, first_hbm, bias_hbm, image_hbm, mask_hbm, pair_ref,
+            t1, t2, t3, spread, order, image, scale, choice,
+            later_ref, first_ref, bias_ref, mask_ref, arrived):
     copies = [
         pltpu.make_async_copy(source, target, arrived.at[i])
         for i, (source, target) in enumerate((
-            (later_hbm, later_ref), (first_hbm, first_ref), (bias_hbm, bias_ref), (image_hbm, image)))
+            (later_hbm, later_ref), (first_hbm, first_ref), (bias_hbm, bias_ref), (image_hbm, image),
+            (mask_hbm, mask_ref)))
     ]
     for copy in copies:
         copy.start()
@@ -62,6 +64,12 @@
     order[WIDTH:, :] = jnp.where(col == 2 * (row % LANES) + row // LANES, 1.0, 0.0).astype(bf16)
     for copy in copies:
         copy.wait()
+    section, pair = lax.axis_index("sec"), pair_ref[0]
+    which = jnp.where(pair == section, 0, jnp.where(pair == (section ^ 1), 1, 2))
+    choice[...] = jnp.broadcast_to(which, choice.shape)
+    mask = jnp.concatenate([mask_ref[...].astype(f32), jnp.zeros((1, LANES - 8), f32)], 1)
+    mask = jnp.transpose(jnp.broadcast_to(mask, (8, LANES)))[0:8, 0:1]
+    scale[...] = jnp.broadcast_to(mask * np.float32(1.0 / np.sqrt(BLK * BLK * C)), scale.shape)
     nothing = jnp.zeros((C, C), f32)
     for layer, t in enumerate((t2, t3)):
         for stream, (even, odd) in enumerate(STREAMS):
@@ -162,8 +170,8 @@
             emit(row + i, r[i * C:(i + 1) * C])
 
 
-def own_features(where, image_ref, t1, t2, t3, spread, order, packed, raw, x1, x2, x3, kept):
-    tile, tiles = where[0], where[1]
+def own_features(image_ref, t1, t2, t3, spread, order, packed, raw, x1, x2, x3, kept):
+    tile, tiles = lax.axis_index("tile"), lax.axis_size("tile")
     pad = JOINT - 1
     kept[:, :, 0:pad * C, :] = jnp.zeros((2, 2, pad * C, WIDTH), bf16)
     kept[:, :, (pad + BLK) * C:, :] = jnp.zeros((2, 2, JOINT * C, WIDTH), bf16)
@@ -189,11 +197,11 @@
                 packed[w, part, y * C:(y + 1) * C, :] = jnp.concatenate(cols, 1)
 
 
-def correlate(where, pair, mask, own_ref, even_ref, odd_ref, t1, t2, t3, spread, order, packed, out_ref,
+def correlate(choice, scale, own_ref, even_ref, odd_ref, t1, t2, t3, spread, order, packed, out_ref,
               raw, x1, x2, x3, feats, turned):
-    tile, tiles, section = where[0], where[1], where[2]
-    image = jnp.where(pair[0] == section, own_ref[...],
-                      jnp.where(pair[0] == (section ^ 1), even_ref[...], odd_ref[...]))
+    tile, tiles = lax.axis_index("tile"), lax.axis_size("tile")
+    which = choice[...]
+    image = jnp.where(which == 0, own_ref[...], jnp.where(which == 1, even_ref[...], odd_ref[...]))
 
     def emit(row, value):
         feats[row * C:(row + 1) * C, :] = value
@@ -257,16 +265,12 @@
                 shift = (SHIFTS * dy - BAND * j) % (3 * LANES)
                 here = (lane >= SHIFTS * dy) & (lane < SHIFTS * (dy + 1))
                 total = jnp.where(here, pltpu.roll(d, shift, 1) if shift else d, total)
-    weight = jnp.zeros((8, 3 * LANES), f32)
-    for b in range(8):
-        weight = jnp.where(iota((8, 3 * LANES), 0) == b, mask[b].astype(f32), weight)
-    total = total * (weight * np.float32(1.0 / np.sqrt(BLK * BLK * C)))
+    total = total * scale[...]
     out_ref[...] = total[:, :SHIFTS * SHIFTS]
 
 
 VMEM = pl.BlockSpec(memory_space=pltpu.VMEM)
 HBM = pl.BlockSpec(memory_space=pltpu.HBM)
-SMEM = pl.BlockSpec(memory_space=pltpu.SMEM)
 
 
 def params(flops, moved, mib=40):
@@ -287,22 +291,25 @@
 
 def body(raw_image, pairing, valid_mask, first_kernel, later_kernels, biases):
     tiles, sections = lax.axis_size("tile"), lax.axis_size("sec")
-    tile, section = lax.axis_index("tile"), lax.axis_index("sec")
+    tile = lax.axis_index("tile")
     image = raw_image[0]
     rows, width = image.shape
     shape = jax.ShapeDtypeStruct
     got_even = lax.ppermute(image, "tile", pairs_even(tiles))
     got_odd = lax.ppermute(image, "tile", pairs_odd(tiles))
-    t1, t2, t3, spread, order, image = pl.pallas_call(
+    t1, t2, t3, spread, order, image, scale, choice = pl.pallas_call(
         prepare,
         out_shape=[shape((512, 192), bf16), shape((2, WIDTH, WIDTH), bf16), shape((2, WIDTH, WIDTH), bf16),
-                   shape((LAYERS, C, WIDTH), f32), shape((2 * WIDTH, WIDTH), bf16), shape(image.shape, f32)],
-        in_specs=[HBM] * 4, out_specs=[VMEM] * 6,
+                   shape((LAYERS, C, WIDTH), f32), shape((2 * WIDTH, WIDTH), bf16), shape(image.shape, f32), shape((8, 3 * LANES), f32),
+                   shape((RAW_ROWS, WIDTH), jnp.int32)],
+        in_specs=[HBM] * 5 + [pl.BlockSpec(memory_space=pltpu.SMEM)], out_specs=[VMEM] * 8,
         scratch_shapes=[pltpu.VMEM((2, 3, 3, C, C), f32), pltpu.VMEM((3, 3, 1, C), f32),
-                        pltpu.VMEM((LAYERS, C), f32), pltpu.SemaphoreType.DMA((4,))],
+                        pltpu.VMEM((LAYERS, C), f32), pltpu.VMEM((1, 8), jnp.int32),
+                        pltpu.SemaphoreType.DMA((5,))],
         name="prepare", **params(10**6, 3 * 10**6),
     )(*(pltpu.with_memory_space_constraint(v, pltpu.HBM) for v in (
-        jnp.transpose(later_kernels, (0, 3, 4, 1, 2)), jnp.transpose(first_kernel, (2, 3, 1, 0)), biases, image)))
+        jnp.transpose(later_kernels, (0, 3, 4, 1, 2)), jnp.transpose(first_kernel, (2, 3, 1, 0)), biases, image,
+        valid_mask[0])), pairing)
 
     odd_tile = (tile % 2) == 1
     above = jnp.where(odd_tile, got_even[rows - HALO:], got_odd[rows - HALO:])
@@ -310,24 +317,23 @@
     own = jnp.concatenate([above, image, below, jnp.zeros((RAW_ROWS - rows - 2 * HALO, width), f32)], 0)
     even = lax.ppermute(own, "sec", pairs_even(sections))
     odd = lax.ppermute(own, "sec", pairs_odd(sections))
-    where = jnp.stack([tile, jnp.int32(tiles), section]).astype(jnp.int32)
     packed = pl.pallas_call(
         own_features,
         out_shape=shape((WIDTH // WIN, 2, DEEP, WIDTH), bf16),
-        in_specs=[SMEM] + [VMEM] * 6, out_specs=VMEM,
+        in_specs=[VMEM] * 6, out_specs=VMEM,
         scratch_shapes=scratch(24, 18, 32) + [pltpu.VMEM((2, 2, (BLK + 2 * JOINT - 1) * C, WIDTH), bf16)],
         name="own_features", **params(5 * 10**9, 10**7),
-    )(where, own, t1, t2, t3, spread, order)
+    )(own, t1, t2, t3, spread, order)
     result = pl.pallas_call(
         correlate,
         out_shape=shape((8, SHIFTS * SHIFTS), f32),
-        in_specs=[SMEM] * 3 + [VMEM] * 9, out_specs=VMEM,
+        in_specs=[VMEM] * 11, out_specs=VMEM,
         scratch_shapes=scratch(32, 26, 48) + [
             pltpu.VMEM(((BLK + 2 * RADIUS) * C, WIDTH), f32),
             pltpu.VMEM((2, WIDTH + 2 * RADIUS, (BLK + 2 * RADIUS + JOINT) * C), bf16),
         ],
         name="correlate", **params(10**10, 10**7),
-    )(where, pairing, valid_mask.reshape(-1), own, even, odd, t1, t2, t3, spread, order, packed)
+    )(choice, scale, own, even, odd, t1, t2, t3, spread, order, packed)
     return result[None, None]
 
 

time: 27.4 us -> 26.4 us (0.964)
  Pallas kernels: 16.1 us -> 15.1 us
    pallas_call x1, Pallas kernels: 9.4 us -> 8.85 us  [body(): pl.pallas_call(correlate, out_shape=shape((8, SHIFTS * SHIFTS), f32), in_...]
    pallas_call x1, Pallas kernels: 4.86 us -> 4.32 us  [body(): pl.pallas_call(own_features, out_shape=shape((WIDTH // WIN, 2, DEEP, WIDT...]
  transfers between devices with their start and end apart: 4 -> 4, of which waited for: 0 -> 0; matrix products, arithmetic and copies ran while one was open for 1% -> 0% of each run, Pallas kernels for 25% -> 24%
where the time goes in v5:
time: 26.4 us; the launch traced here: 26.2 us
  Pallas kernels  15.1 us (57%)
  starting transfers between devices  10.1 us (38%)
  between operations  0.73 us (3%)
    pallas_call x1, Pallas kernels, body(): pl.pallas_call(correlate, out_shape=shape((8, SHIFTS * SHIFTS), f32), in_...  8.85 us
    ppermute x1, starting transfers between devices, body(): got_even = lax.ppermute(image, 'tile', pairs_even(tiles))  5.91 us
    pallas_call x1, Pallas kernels, body(): pl.pallas_call(own_features, out_shape=shape((WIDTH // WIN, 2, DEEP, WIDT...  4.32 us
    ppermute x1, starting transfers between devices, body(): even = lax.ppermute(own, 'sec', pairs_even(sections))  2.92 us
    pallas_call x1, Pallas kernels, body(): pl.pallas_call(prepare, out_shape=[shape((512, 192), bf16), shape((2, WID...  1.96 us
    ppermute x1, starting transfers between devices, body(): odd = lax.ppermute(own, 'sec', pairs_odd(sections))  0.65 us
    ppermute x1, starting transfers between devices, body(): got_odd = lax.ppermute(image, 'tile', pairs_odd(tiles))  0.65 us
  transfers between devices with their start and end apart: 4, of which 0 were waited for; matrix products, arithmetic and copies ran while one was open for 0% of the time, Pallas kernels for 24%

profile of v5, /device:TPU:0, one launch (start us, length us, event | category | flops | bytes accessed | tf_op | source)
XLA Modules:
  0.0 26.2 jit_solution(11173671043001836326)
XLA Ops:
  0.0 0.7 %collective-permute-start.1 = (f32[32,256]{1,0:T(8,128)}, f32[32,256]{1,0:T(8,128)S(1)}, u32[]{:S(2)}, u32[]{:S(2)}) collective-permute-start(f32[32,256]{1,0:T(8,128)} %bitcast.6), channel_id=1, source_target_pairs={{1,2},{2,1},{5,6},{6,5},{9,10},{10,9},{13,14},{14,13},{17,18},{18,... | collective-permute-start | bytes 98312 | tf_op jit(solution)/shard_map/ppermute | solution.py:299
  0.7 5.9 %collective-permute-start = (f32[32,256]{1,0:T(8,128)}, f32[32,256]{1,0:T(8,128)S(1)}, u32[]{:S(2)}, u32[]{:S(2)}) collective-permute-start(f32[32,256]{1,0:T(8,128)} %bitcast.7), channel_id=1, source_target_pairs={{0,1},{1,0},{2,3},{3,2},{4,5},{5,4},{6,7},{7,6},{8,9},{9,8},{10,11... | collective-permute-start | bytes 98312 | tf_op jit(solution)/shard_map/ppermute | solution.py:298
  7.2 0.1 pad.3.clone
  7.3 2.0 %prepare.1 = (bf16[512,192]{1,0:T(8,128)(2,1)S(1)}, bf16[2,256,256]{2,1,0:T(8,128)(2,1)S(1)}, bf16[2,256,256]{2,1,0:T(8,128)(2,1)S(1)}, f32[3,32,256]{2,1,0:T(8,...) custom-call(f32[2,3,3,32,32]{4,3,2,1,0:T(8,128)} %bitcast.5, ...), custom_call_target="tpu_custom_call" | custom-call | flops 1000000 | bytes 3000000 | tf_op jit(solution)/shard_map/prepare/pallas_call | solution.py:300
  9.3 0.0 collective-permute-done.1
  9.3 0.0 collective-permute-done
  9.3 0.1 maximum_maximum_fusion.image_ref.own_ref
  9.4 0.7 %collective-permute-start.3 = (f32[64,256]{1,0:T(8,128)S(1)}, f32[64,256]{1,0:T(8,128)S(1)}, u32[]{:S(2)}, u32[]{:S(2)}) collective-permute-start(f32[64,256]{1,0:T(8,128)S(1)} %maximum_maximum_fusion.image_ref.own_ref), channel_id=1, source_target_pairs={{4,8},{8,4},{5,9},{9,5},{6,10},{10,6},{7,11},{11,7},{20,24},{24,20... | collective-permute-start | bytes 196616 | tf_op jit(solution)/shard_map/ppermute | solution.py:319
  10.1 2.9 %collective-permute-start.2 = (f32[64,256]{1,0:T(8,128)S(1)}, f32[64,256]{1,0:T(8,128)S(1)}, u32[]{:S(2)}, u32[]{:S(2)}) collective-permute-start(f32[64,256]{1,0:T(8,128)S(1)} %maximum_maximum_fusion.image_ref.own_ref), channel_id=1, source_target_pairs={{0,4},{4,0},{8,12},{12,8},{1,5},{5,1},{9,13},{13,9},{2,6},{6,2},{1... | collective-permute-start | bytes 196616 | tf_op jit(solution)/shard_map/ppermute | solution.py:318
  13.0 4.3 %own_features.1.packed = bf16[4,2,1152,256]{3,2,1,0:T(8,128)(2,1)S(1)} custom-call(f32[64,256]{1,0:T(8,128)S(1)} %maximum_maximum_fusion.image_ref.own_ref, bf16[512,192]{1,0:T(8,128)(2,1)S(1)} %get-tuple-element.16.t1, bf16[2,256,256]{2,1,0:T(8,128)(2,1)S(1)} %get-tuple-element.17.t2, bf16[2,256,256]{2,1,0:T(8,128)(2,1)S(1)} %get-tuple-element.18.t3, ...), custom_call_target="tpu_custom_call" | custom-call | flops 5000000000 | bytes 10000000 | tf_op jit(solution)/shard_map/own_features/pallas_call | solution.py:320
  17.3 0.0 collective-permute-done.3.odd_ref
  17.3 0.0 collective-permute-done.2.even_ref
  17.3 8.8 %correlate.1 = f32[8,289]{1,0:T(8,128)} custom-call(s32[64,256]{1,0:T(8,128)S(1)} %get-tuple-element.13.choice, f32[8,384]{1,0:T(8,128)S(1)} %get-tuple-element.14.scale, f32[64,256]{1,0:T(8,128)S(1)} %maximum_maximum_fusion.image_ref.own_ref, f32[64,256]{1,0:T(8,128)S(1)} %collective-permute-done.2.even_ref, f32[64,256]{1,0:T(8,128)S(1)} %collective-permute-done.3.odd_ref, ...), custom_call_target="tpu_custom_call" | custom-call | flops 10000000000 | bytes 10000000 | tf_op jit(solution)/shard_map/correlate/pallas_call | solution.py:327
  (2 shorter events, 0.0 us)
Async XLA Ops:
  0.0 9.3 %collective-permute-start.1 = (f32[32,256]{1,0:T(8,128)}, f32[32,256]{1,0:T(8,128)S(1)}, u32[]{:S(2)}, u32[]{:S(2)}) collective-permute-start(f32[32,256]{1,0:T(8,128)} %bitcast.6), channel_id=1, source_target_pairs={{1,2},{2,1},{5,6},{6,5},{9,10},{10,9},{13,14},{14,13},{17,18},{18,... | collective-permute-start | bytes 98312 | tf_op jit(solution)/shard_map/ppermute | solution.py:299
  0.7 8.6 %collective-permute-start = (f32[32,256]{1,0:T(8,128)}, f32[32,256]{1,0:T(8,128)S(1)}, u32[]{:S(2)}, u32[]{:S(2)}) collective-permute-start(f32[32,256]{1,0:T(8,128)} %bitcast.7), channel_id=1, source_target_pairs={{0,1},{1,0},{2,3},{3,2},{4,5},{5,4},{6,7},{7,6},{8,9},{9,8},{10,11... | collective-permute-start | bytes 98312 | tf_op jit(solution)/shard_map/ppermute | solution.py:298
  9.4 7.9 %collective-permute-start.3 = (f32[64,256]{1,0:T(8,128)S(1)}, f32[64,256]{1,0:T(8,128)S(1)}, u32[]{:S(2)}, u32[]{:S(2)}) collective-permute-start(f32[64,256]{1,0:T(8,128)S(1)} %maximum_maximum_fusion.image_ref.own_ref), channel_id=1, source_target_pairs={{4,8},{8,4},{5,9},{9,5},{6,10},{10,6},{7,11},{11,7},{20,24},{24,20... | collective-permute-start | bytes 196616 | tf_op jit(solution)/shard_map/ppermute | solution.py:319
  10.1 7.3 %collective-permute-start.2 = (f32[64,256]{1,0:T(8,128)S(1)}, f32[64,256]{1,0:T(8,128)S(1)}, u32[]{:S(2)}, u32[]{:S(2)}) collective-permute-start(f32[64,256]{1,0:T(8,128)S(1)} %maximum_maximum_fusion.image_ref.own_ref), channel_id=1, source_target_pairs={{0,4},{4,0},{8,12},{12,8},{1,5},{5,1},{9,13},{13,9},{2,6},{6,2},{1... | collective-permute-start | bytes 196616 | tf_op jit(solution)/shard_map/ppermute | solution.py:318

commit v6 on v5

--- a/solution.py
+++ b/solution.py
@@ -160,9 +160,15 @@
             for run in range(2):
                 rows = slice((run * n3 + row) * C, (run * n3 + row + 1) * C)
                 for parity, v in enumerate((a, b)):
-                    high, low = split(v[:, run * LANES:(run + 1) * LANES])
+                    half = v[:, run * LANES:(run + 1) * LANES]
+                    if x3 is None:
+                        emit(run * n3 + row, parity, half)
+                        continue
+                    high, low = split(half)
                     x3[rows, parity * LANES:(parity + 1) * LANES] = high
                     x3[rows, WIDTH + parity * LANES:WIDTH + (parity + 1) * LANES] = low
+    if x3 is None:
+        return
     together = jnp.concatenate([order[WIDTH:, :]] * 2, 0)
     for row in range(0, 2 * n3, 16):
         r = dot(x3[row * C:(row + 16) * C, :], together)
@@ -170,7 +176,7 @@
             emit(row + i, r[i * C:(i + 1) * C])
 
 
-def own_features(image_ref, t1, t2, t3, spread, order, packed, raw, x1, x2, x3, kept):
+def own_features(image_ref, t1, t2, t3, spread, order, kept, raw, x1, x2, x3):
     tile, tiles = lax.axis_index("tile"), lax.axis_size("tile")
     pad = JOINT - 1
     kept[:, :, 0:pad * C, :] = jnp.zeros((2, 2, pad * C, WIDTH), bf16)
@@ -184,45 +190,52 @@
 
     encode(image_ref[...], (8, 24), (3, 9, 8), (2, 18, 1, 17), tile, tiles,
            t1, t2, t3, spread, order, raw, x1, x2, x3, emit)
+
+
+def joined(kept, w, part):
     left = iota((C, LANES), 1) < WIN
-    for w in range(WIDTH // WIN):
-        half = slice((w // 2) * LANES, (w // 2 + 1) * LANES)
-        for part in range(2):
-            for y in range(BLK + JOINT):
-                cols = []
-                for g in (0, 2):
-                    a = kept[w % 2, part, (y - g + pad) * C:(y - g + pad + 1) * C, half]
-                    b = kept[1 - w % 2, part, (y - g - 1 + pad) * C:(y - g + pad) * C, half]
-                    cols.append(jnp.where(left, a, b))
-                packed[w, part, y * C:(y + 1) * C, :] = jnp.concatenate(cols, 1)
-
-
-def correlate(choice, scale, own_ref, even_ref, odd_ref, t1, t2, t3, spread, order, packed, out_ref,
-              raw, x1, x2, x3, feats, turned):
+    half = slice((w // 2) * LANES, (w // 2 + 1) * LANES)
+    rows = []
+    for y in range(BLK + JOINT):
+        at = y + JOINT - 1
+        cols = []
+        for g in (0, 2):
+            a = kept[w % 2, part, (at - g) * C:(at - g + 1) * C, half]
+            b = kept[1 - w % 2, part, (at - g - 1) * C:(at - g) * C, half]
+            cols.append(jnp.where(left, a, b))
+        rows.append(jnp.concatenate(cols, 1))
+    return jnp.concatenate(rows, 0)
+
+
+def correlate(choice, scale, own_ref, even_ref, odd_ref, t1, t2, t3, spread, order, kept, out_ref,
+              raw, x1, x2, feats, mixed, turned):
     tile, tiles = lax.axis_index("tile"), lax.axis_size("tile")
     which = choice[...]
     image = jnp.where(which == 0, own_ref[...], jnp.where(which == 1, even_ref[...], odd_ref[...]))
 
-    def emit(row, value):
-        feats[row * C:(row + 1) * C, :] = value
+    def emit(row, parity, half):
+        feats[parity, row * C:(row + 1) * C, :] = half
 
     encode(image, (0, 24), (4, 13, 12), (10, 18, 9, 17), tile, tiles,
-           t1, t2, t3, spread, order, raw, x1, x2, x3, emit)
+           t1, t2, t3, spread, order, raw, x1, x2, None, emit)
 
     @pl.when(tile == 0)
     def _():
-        feats[0:RADIUS * C, :] = jnp.zeros((RADIUS * C, WIDTH), f32)
+        feats[:, 0:RADIUS * C, :] = jnp.zeros((2, RADIUS * C, LANES), f32)
 
     @pl.when(tile == tiles - 1)
     def _():
-        feats[(BLK + RADIUS) * C:, :] = jnp.zeros((RADIUS * C, WIDTH), f32)
+        feats[:, (BLK + RADIUS) * C:, :] = jnp.zeros((2, RADIUS * C, LANES), f32)
 
     border = jnp.zeros((RADIUS, LANES), f32)
     turned[:, :, (BLK + 2 * RADIUS) * C:] = jnp.zeros((2, WIDTH + 2 * RADIUS, JOINT * C), bf16)
     for q in range((BLK + 2 * RADIUS) * C // LANES):
         cols = slice(q * LANES, (q + 1) * LANES)
-        v = jnp.concatenate([border, jnp.transpose(feats[cols, :]), border], 0)
-        turned[0, :, cols], turned[1, :, cols] = split(v)
+        for parity in range(2):
+            mixed[q, pl.ds(RADIUS + parity, LANES, stride=2), :] = jnp.transpose(feats[parity, cols, :])
+        mixed[q, 0:RADIUS, :] = border
+        mixed[q, RADIUS + WIDTH:, :] = border
+        turned[0, :, cols], turned[1, :, cols] = split(mixed[q])
 
     lane8, sub8 = iota((8, LANES), 1), iota((8, LANES), 0)
     eighth = (iota((8, WIDTH), 1) % WIN) // 8
@@ -234,7 +247,8 @@
             cols = slice(j * JOINT * C, j * JOINT * C + DEEP)
             high, low = turned[0, rows, cols], turned[1, rows, cols]
             lefts.append(jnp.concatenate([high, low, high], 1))
-        right = jnp.concatenate([packed[w, 0], packed[w, 0], packed[w, 1]], 0)
+        high, low = joined(kept, w, 0), joined(kept, w, 1)
+        right = jnp.concatenate([high, high, low], 0)
         p = dot(jnp.concatenate(lefts, 0), right)
         bands = []
         for j in range(STEPS):
@@ -317,23 +331,24 @@
     own = jnp.concatenate([above, image, below, jnp.zeros((RAW_ROWS - rows - 2 * HALO, width), f32)], 0)
     even = lax.ppermute(own, "sec", pairs_even(sections))
     odd = lax.ppermute(own, "sec", pairs_odd(sections))
-    packed = pl.pallas_call(
+    kept = pl.pallas_call(
         own_features,
-        out_shape=shape((WIDTH // WIN, 2, DEEP, WIDTH), bf16),
+        out_shape=shape((2, 2, (BLK + 2 * JOINT - 1) * C, WIDTH), bf16),
         in_specs=[VMEM] * 6, out_specs=VMEM,
-        scratch_shapes=scratch(24, 18, 32) + [pltpu.VMEM((2, 2, (BLK + 2 * JOINT - 1) * C, WIDTH), bf16)],
+        scratch_shapes=scratch(24, 18, 32),
         name="own_features", **params(5 * 10**9, 10**7),
     )(own, t1, t2, t3, spread, order)
     result = pl.pallas_call(
         correlate,
         out_shape=shape((8, SHIFTS * SHIFTS), f32),
         in_specs=[VMEM] * 11, out_specs=VMEM,
-        scratch_shapes=scratch(32, 26, 48) + [
-            pltpu.VMEM(((BLK + 2 * RADIUS) * C, WIDTH), f32),
+        scratch_shapes=scratch(32, 26, 0)[:3] + [
+            pltpu.VMEM((2, (BLK + 2 * RADIUS) * C, LANES), f32),
+            pltpu.VMEM(((BLK + 2 * RADIUS) * C // LANES, WIDTH + 2 * RADIUS, LANES), f32),
             pltpu.VMEM((2, WIDTH + 2 * RADIUS, (BLK + 2 * RADIUS + JOINT) * C), bf16),
         ],
         name="correlate", **params(10**10, 10**7),
-    )(choice, scale, own, even, odd, t1, t2, t3, spread, order, packed)
+    )(choice, scale, own, even, odd, t1, t2, t3, spread, order, kept)
     return result[None, None]
 
 

time: 26.4 us -> 25.3 us (0.958)
  Pallas kernels: 15.1 us -> 14.1 us
    pallas_call x1, Pallas kernels: 4.32 us -> 3.64 us  [body(): pl.pallas_call(own_features, out_shape=shape((2, 2, (BLK + 2 * JOINT - 1)...]
    pallas_call x1, Pallas kernels: 8.85 us -> 8.51 us  [body(): pl.pallas_call(correlate, out_shape=shape((8, SHIFTS * SHIFTS), f32), in_...]
  transfers between devices with their start and end apart: 4 -> 4, of which waited for: 0 -> 0; matrix products, arithmetic and copies ran while one was open for 0% -> 0% of each run, Pallas kernels for 24% -> 22%
where the time goes in v6:
time: 25.3 us; the launch traced here: 25.1 us
  Pallas kernels  14.1 us (56%)
  starting transfers between devices  10.1 us (40%)
  between operations  0.73 us (3%)
    pallas_call x1, Pallas kernels, body(): pl.pallas_call(correlate, out_shape=shape((8, SHIFTS * SHIFTS), f32), in_...  8.51 us
    ppermute x1, starting transfers between devices, body(): got_even = lax.ppermute(image, 'tile', pairs_even(tiles))  5.91 us
    pallas_call x1, Pallas kernels, body(): pl.pallas_call(own_features, out_shape=shape((2, 2, (BLK + 2 * JOINT - 1)...  3.64 us
    ppermute x1, starting transfers between devices, body(): even = lax.ppermute(own, 'sec', pairs_even(sections))  2.92 us
    pallas_call x1, Pallas kernels, body(): pl.pallas_call(prepare, out_shape=[shape((512, 192), bf16), shape((2, WID...  1.96 us
    ppermute x1, starting transfers between devices, body(): odd = lax.ppermute(own, 'sec', pairs_odd(sections))  0.65 us
    ppermute x1, starting transfers between devices, body(): got_odd = lax.ppermute(image, 'tile', pairs_odd(tiles))  0.65 us
  transfers between devices with their start and end apart: 4, of which 0 were waited for; matrix products, arithmetic and copies ran while one was open for 0% of the time, Pallas kernels for 22%

profile of v6, /device:TPU:0, one launch (start us, length us, event | category | flops | bytes accessed | tf_op | source)
XLA Modules:
  0.0 25.1 jit_solution(2102903322374624174)
XLA Ops:
  0.0 0.7 %collective-permute-start.1 = (f32[32,256]{1,0:T(8,128)}, f32[32,256]{1,0:T(8,128)S(1)}, u32[]{:S(2)}, u32[]{:S(2)}) collective-permute-start(f32[32,256]{1,0:T(8,128)} %bitcast.6), channel_id=1, source_target_pairs={{1,2},{2,1},{5,6},{6,5},{9,10},{10,9},{13,14},{14,13},{17,18},{18,... | collective-permute-start | bytes 98312 | tf_op jit(solution)/shard_map/ppermute | solution.py:313
  0.7 5.9 %collective-permute-start = (f32[32,256]{1,0:T(8,128)}, f32[32,256]{1,0:T(8,128)S(1)}, u32[]{:S(2)}, u32[]{:S(2)}) collective-permute-start(f32[32,256]{1,0:T(8,128)} %bitcast.7), channel_id=1, source_target_pairs={{0,1},{1,0},{2,3},{3,2},{4,5},{5,4},{6,7},{7,6},{8,9},{9,8},{10,11... | collective-permute-start | bytes 98312 | tf_op jit(solution)/shard_map/ppermute | solution.py:312
  7.2 0.1 pad.3.clone
  7.3 2.0 %prepare.1 = (bf16[512,192]{1,0:T(8,128)(2,1)S(1)}, bf16[2,256,256]{2,1,0:T(8,128)(2,1)S(1)}, bf16[2,256,256]{2,1,0:T(8,128)(2,1)S(1)}, f32[3,32,256]{2,1,0:T(8,...) custom-call(f32[2,3,3,32,32]{4,3,2,1,0:T(8,128)} %bitcast.5, ...), custom_call_target="tpu_custom_call" | custom-call | flops 1000000 | bytes 3000000 | tf_op jit(solution)/shard_map/prepare/pallas_call | solution.py:314
  9.3 0.0 collective-permute-done.1
  9.3 0.0 collective-permute-done
  9.3 0.1 maximum_maximum_fusion.image_ref.own_ref
  9.4 0.7 %collective-permute-start.3 = (f32[64,256]{1,0:T(8,128)S(1)}, f32[64,256]{1,0:T(8,128)S(1)}, u32[]{:S(2)}, u32[]{:S(2)}) collective-permute-start(f32[64,256]{1,0:T(8,128)S(1)} %maximum_maximum_fusion.image_ref.own_ref), channel_id=1, source_target_pairs={{4,8},{8,4},{5,9},{9,5},{6,10},{10,6},{7,11},{11,7},{20,24},{24,20... | collective-permute-start | bytes 196616 | tf_op jit(solution)/shard_map/ppermute | solution.py:333
  10.1 2.9 %collective-permute-start.2 = (f32[64,256]{1,0:T(8,128)S(1)}, f32[64,256]{1,0:T(8,128)S(1)}, u32[]{:S(2)}, u32[]{:S(2)}) collective-permute-start(f32[64,256]{1,0:T(8,128)S(1)} %maximum_maximum_fusion.image_ref.own_ref), channel_id=1, source_target_pairs={{0,4},{4,0},{8,12},{12,8},{1,5},{5,1},{9,13},{13,9},{2,6},{6,2},{1... | collective-permute-start | bytes 196616 | tf_op jit(solution)/shard_map/ppermute | solution.py:332
  13.0 3.6 %own_features.1.kept = bf16[2,2,1248,256]{3,2,1,0:T(8,128)(2,1)S(1)} custom-call(f32[64,256]{1,0:T(8,128)S(1)} %maximum_maximum_fusion.image_ref.own_ref, bf16[512,192]{1,0:T(8,128)(2,1)S(1)} %get-tuple-element.16.t1, bf16[2,256,256]{2,1,0:T(8,128)(2,1)S(1)} %get-tuple-element.17.t2, bf16[2,256,256]{2,1,0:T(8,128)(2,1)S(1)} %get-tuple-element.18.t3, ...), custom_call_target="tpu_custom_call" | custom-call | flops 5000000000 | bytes 10000000 | tf_op jit(solution)/shard_map/own_features/pallas_call | solution.py:334
  16.6 0.0 collective-permute-done.3.odd_ref
  16.6 0.0 collective-permute-done.2.even_ref
  16.6 8.5 %correlate.1 = f32[8,289]{1,0:T(8,128)} custom-call(s32[64,256]{1,0:T(8,128)S(1)} %get-tuple-element.13.choice, f32[8,384]{1,0:T(8,128)S(1)} %get-tuple-element.14.scale, f32[64,256]{1,0:T(8,128)S(1)} %maximum_maximum_fusion.image_ref.own_ref, f32[64,256]{1,0:T(8,128)S(1)} %collective-permute-done.2.even_ref, f32[64,256]{1,0:T(8,128)S(1)} %collective-permute-done.3.odd_ref, ...), custom_call_target="tpu_custom_call" | custom-call | flops 10000000000 | bytes 10000000 | tf_op jit(solution)/shard_map/correlate/pallas_call | solution.py:341
  (2 shorter events, 0.0 us)
Async XLA Ops:
  0.0 9.3 %collective-permute-start.1 = (f32[32,256]{1,0:T(8,128)}, f32[32,256]{1,0:T(8,128)S(1)}, u32[]{:S(2)}, u32[]{:S(2)}) collective-permute-start(f32[32,256]{1,0:T(8,128)} %bitcast.6), channel_id=1, source_target_pairs={{1,2},{2,1},{5,6},{6,5},{9,10},{10,9},{13,14},{14,13},{17,18},{18,... | collective-permute-start | bytes 98312 | tf_op jit(solution)/shard_map/ppermute | solution.py:313
  0.7 8.6 %collective-permute-start = (f32[32,256]{1,0:T(8,128)}, f32[32,256]{1,0:T(8,128)S(1)}, u32[]{:S(2)}, u32[]{:S(2)}) collective-permute-start(f32[32,256]{1,0:T(8,128)} %bitcast.7), channel_id=1, source_target_pairs={{0,1},{1,0},{2,3},{3,2},{4,5},{5,4},{6,7},{7,6},{8,9},{9,8},{10,11... | collective-permute-start | bytes 98312 | tf_op jit(solution)/shard_map/ppermute | solution.py:312
  9.4 7.2 %collective-permute-start.3 = (f32[64,256]{1,0:T(8,128)S(1)}, f32[64,256]{1,0:T(8,128)S(1)}, u32[]{:S(2)}, u32[]{:S(2)}) collective-permute-start(f32[64,256]{1,0:T(8,128)S(1)} %maximum_maximum_fusion.image_ref.own_ref), channel_id=1, source_target_pairs={{4,8},{8,4},{5,9},{9,5},{6,10},{10,6},{7,11},{11,7},{20,24},{24,20... | collective-permute-start | bytes 196616 | tf_op jit(solution)/shard_map/ppermute | solution.py:333
  10.1 6.6 %collective-permute-start.2 = (f32[64,256]{1,0:T(8,128)S(1)}, f32[64,256]{1,0:T(8,128)S(1)}, u32[]{:S(2)}, u32[]{:S(2)}) collective-permute-start(f32[64,256]{1,0:T(8,128)S(1)} %maximum_maximum_fusion.image_ref.own_ref), channel_id=1, source_target_pairs={{0,4},{4,0},{8,12},{12,8},{1,5},{5,1},{9,13},{13,9},{2,6},{6,2},{1... | collective-permute-start | bytes 196616 | tf_op jit(solution)/shard_map/ppermute | solution.py:332

commit v7 on v6

--- a/solution.py
+++ b/solution.py
@@ -89,7 +89,7 @@
         piece = jnp.zeros(shape, f32)
         for ky in range(3):
             pair = [jnp.zeros((1, C), f32) if kx is None else first_ref[ky, kx] for kx in (even, odd)]
-            piece = jnp.where(offset == ky, jnp.broadcast_to(jnp.concatenate(pair * 8, 1), shape), piece)
+            piece = jnp.where(offset == ky, jnp.broadcast_to(jnp.concatenate([jnp.concatenate(pair * 2, 1)] * 4, 1), shape), piece)
         pieces.append(piece)
     pieces.append(jnp.zeros((64, 8 * 2 * C), f32))
     high, low = split(jnp.transpose(jnp.concatenate(pieces, 0)))
@@ -103,7 +103,7 @@
 
 
 def encode(image, starts, groups, ends, tile, tiles, t1, t2, t3, spread, order, raw, x1, x2, x3, emit):
-    n1, n2, n3 = 8 * groups[0], 2 * groups[1], 2 * groups[2]
+    n1, n2, n3 = groups[0], 2 * groups[1], 2 * groups[2]
     h = image.astype(bf16)
     rest = image - h.astype(f32)
     m = rest.astype(bf16)
@@ -115,7 +115,7 @@
     before = jnp.where(col == 0, 0.0, pltpu.roll(odd, 1, 1))
     after = jnp.where(col == LANES - 1, 0.0, pltpu.roll(even, LANES - 1, 1))
     for form, v in enumerate((even, odd, before, after)):
-        raw[form] = jnp.concatenate([v[a:a + n1 + 8] for a in starts], 1)
+        raw[form] = jnp.concatenate([v[a:a + raw.shape[1]] for a in starts], 1)
     lane = iota((C, WIDTH), 1) % LANES
     twice = lambda v: jnp.concatenate([v, v], 0)
 
@@ -145,10 +145,11 @@
             a, b, c, d = (r[(yo * 4 + i) * C:(yo * 4 + i + 1) * C] for i in range(4))
             yield 2 * step + yo, a + shifted(b, 1, 0) + bias, c + shifted(d, LANES - 1, LANES - 1) + bias
 
-    for g in range(groups[0]):
+    for g in range((n1 + 7) // 8):
+        count = min(8, n1 - 8 * g)
         high, low = split(jnp.concatenate([raw[form, 8 * g:8 * g + 16, :] for form in range(4)], 0))
-        r = dot(t1[...], jnp.concatenate([high, high, low], 0))
-        for yo in range(8):
+        r = dot(t1[0:count * 2 * C, :], jnp.concatenate([high, high, low], 0))
+        for yo in range(count):
             put(x1, 8 * g + yo, jnp.tanh(r[yo * 2 * C:(yo + 1) * 2 * C] + twice(spread[0])))
     outside(x1, ends[0], ends[1], n1)
     for step in range(groups[1]):
@@ -188,7 +189,7 @@
         for form, v in enumerate((value, jnp.concatenate(turned, 1))):
             kept[form, 0, rows, :], kept[form, 1, rows, :] = split(v)
 
-    encode(image_ref[...], (8, 24), (3, 9, 8), (2, 18, 1, 17), tile, tiles,
+    encode(image_ref[...], (8, 24), (20, 9, 8), (2, 18, 1, 17), tile, tiles,
            t1, t2, t3, spread, order, raw, x1, x2, x3, emit)
 
 
@@ -213,29 +214,33 @@
     which = choice[...]
     image = jnp.where(which == 0, own_ref[...], jnp.where(which == 1, even_ref[...], odd_ref[...]))
 
+    border = jnp.zeros((RADIUS, LANES), f32)
+    deep = (BLK + 2 * RADIUS) * C
+    turned[:, :, deep:] = jnp.zeros((2, WIDTH + 2 * RADIUS, JOINT * C), bf16)
+
     def emit(row, parity, half):
         feats[parity, row * C:(row + 1) * C, :] = half
-
-    encode(image, (0, 24), (4, 13, 12), (10, 18, 9, 17), tile, tiles,
-           t1, t2, t3, spread, order, raw, x1, x2, None, emit)
-
-    @pl.when(tile == 0)
-    def _():
-        feats[:, 0:RADIUS * C, :] = jnp.zeros((2, RADIUS * C, LANES), f32)
-
-    @pl.when(tile == tiles - 1)
-    def _():
-        feats[:, (BLK + RADIUS) * C:, :] = jnp.zeros((2, RADIUS * C, LANES), f32)
-
-    border = jnp.zeros((RADIUS, LANES), f32)
-    turned[:, :, (BLK + 2 * RADIUS) * C:] = jnp.zeros((2, WIDTH + 2 * RADIUS, JOINT * C), bf16)
-    for q in range((BLK + 2 * RADIUS) * C // LANES):
+        if row % 4 < 3 or parity == 0:
+            return
+        q = row // 4
         cols = slice(q * LANES, (q + 1) * LANES)
-        for parity in range(2):
-            mixed[q, pl.ds(RADIUS + parity, LANES, stride=2), :] = jnp.transpose(feats[parity, cols, :])
+        for p in range(2):
+            mixed[q, pl.ds(RADIUS + p, LANES, stride=2), :] = jnp.transpose(feats[p, cols, :])
         mixed[q, 0:RADIUS, :] = border
         mixed[q, RADIUS + WIDTH:, :] = border
         turned[0, :, cols], turned[1, :, cols] = split(mixed[q])
+
+    encode(image, (0, 24), (28, 13, 12), (10, 18, 9, 17), tile, tiles,
+           t1, t2, t3, spread, order, raw, x1, x2, None, emit)
+    beyond = jnp.zeros((2, WIDTH + 2 * RADIUS, RADIUS * C), bf16)
+
+    @pl.when(tile == 0)
+    def _():
+        turned[:, :, 0:RADIUS * C] = beyond
+
+    @pl.when(tile == tiles - 1)
+    def _():
+        turned[:, :, deep - RADIUS * C:deep] = beyond
 
     lane8, sub8 = iota((8, LANES), 1), iota((8, LANES), 0)
     eighth = (iota((8, WIDTH), 1) % WIN) // 8
@@ -296,7 +301,7 @@
 
 def scratch(rows1, rows2, rows3):
     return [
-        pltpu.VMEM((4, rows1 + 8, WIDTH), f32),
+        pltpu.VMEM((4, (rows1 + 7) // 8 * 8 + 8, WIDTH), f32),
         pltpu.VMEM((2, rows1 * 2 * C, WIDTH), bf16),
         pltpu.VMEM((2, rows2 * 2 * C, WIDTH), bf16),
         pltpu.VMEM((rows3 * C, 2 * WIDTH), bf16),
@@ -325,9 +330,9 @@
         jnp.transpose(later_kernels, (0, 3, 4, 1, 2)), jnp.transpose(first_kernel, (2, 3, 1, 0)), biases, image,
         valid_mask[0])), pairing)
 
-    odd_tile = (tile % 2) == 1
-    above = jnp.where(odd_tile, got_even[rows - HALO:], got_odd[rows - HALO:])
-    below = jnp.where(odd_tile, got_odd[:HALO], got_even[:HALO])
+    even_tile = (tile % 2) == 0
+    below = jnp.where(even_tile, got_even[:HALO], got_odd[:HALO])
+    above = jnp.where(even_tile, got_odd[rows - HALO:], got_even[rows - HALO:])
     own = jnp.concatenate([above, image, below, jnp.zeros((RAW_ROWS - rows - 2 * HALO, width), f32)], 0)
     even = lax.ppermute(own, "sec", pairs_even(sections))
     odd = lax.ppermute(own, "sec", pairs_odd(sections))
@@ -335,14 +340,14 @@
         own_features,
         out_shape=shape((2, 2, (BLK + 2 * JOINT - 1) * C, WIDTH), bf16),
         in_specs=[VMEM] * 6, out_specs=VMEM,
-        scratch_shapes=scratch(24, 18, 32),
+        scratch_shapes=scratch(20, 18, 32),
         name="own_features", **params(5 * 10**9, 10**7),
     )(own, t1, t2, t3, spread, order)
     result = pl.pallas_call(
         correlate,
         out_shape=shape((8, SHIFTS * SHIFTS), f32),
         in_specs=[VMEM] * 11, out_specs=VMEM,
-        scratch_shapes=scratch(32, 26, 0)[:3] + [
+        scratch_shapes=scratch(28, 26, 0)[:3] + [
             pltpu.VMEM((2, (BLK + 2 * RADIUS) * C, LANES), f32),
             pltpu.VMEM(((BLK + 2 * RADIUS) * C // LANES, WIDTH + 2 * RADIUS, LANES), f32),
             pltpu.VMEM((2, WIDTH + 2 * RADIUS, (BLK + 2 * RADIUS + JOINT) * C), bf16),

time: 25.3 us -> 23.8 us (0.941)
  the two profiles are of different devices: /device:TPU:0 before, /device:TPU:9 now
where the time goes in v7:
time: 23.8 us; the launch traced here: 23.6 us
  Pallas kernels  13.9 us (58%)
  starting transfers between devices  8.79 us (37%)
  between operations  0.75 us (3%)
    pallas_call x1, Pallas kernels, body(): pl.pallas_call(correlate, out_shape=shape((8, SHIFTS * SHIFTS), f32), in_...  8.4 us
    ppermute x1, starting transfers between devices, body(): got_odd = lax.ppermute(image, 'tile', pairs_odd(tiles))  4.49 us
    ppermute x1, starting transfers between devices, body(): odd = lax.ppermute(own, 'sec', pairs_odd(sections))  4.23 us
    pallas_call x1, Pallas kernels, body(): pl.pallas_call(own_features, out_shape=shape((2, 2, (BLK + 2 * JOINT - 1)...  3.54 us
    pallas_call x1, Pallas kernels, body(): pl.pallas_call(prepare, out_shape=[shape((512, 192), bf16), shape((2, WID...  1.96 us
  transfers between devices with their start and end apart: 4, of which 0 were waited for; matrix products, arithmetic and copies ran while one was open for 0% of the time, Pallas kernels for 23%

profile of v7, /device:TPU:9, one launch (start us, length us, event | category | flops | bytes accessed | tf_op | source)
XLA Modules:
  0.0 23.6 jit_solution(5651458480119786110)
XLA Ops:
  0.0 0.0 collective-permute-start.1
  0.0 4.5 %collective-permute-start = (f32[32,256]{1,0:T(8,128)}, f32[32,256]{1,0:T(8,128)S(1)}, u32[]{:S(2)}, u32[]{:S(2)}) collective-permute-start(f32[32,256]{1,0:T(8,128)} %bitcast.7), channel_id=1, source_target_pairs={{1,2},{2,1},{5,6},{6,5},{9,10},{10,9},{13,14},{14,13},{17,18},{18,... | collective-permute-start | bytes 98312 | tf_op jit(solution)/shard_map/ppermute | solution.py:318
  5.2 0.1 pad.3.clone
  5.2 2.0 %prepare.1 = (bf16[512,192]{1,0:T(8,128)(2,1)S(1)}, bf16[2,256,256]{2,1,0:T(8,128)(2,1)S(1)}, bf16[2,256,256]{2,1,0:T(8,128)(2,1)S(1)}, f32[3,32,256]{2,1,0:T(8,...) custom-call(f32[2,3,3,32,32]{4,3,2,1,0:T(8,128)} %bitcast.5, ...), custom_call_target="tpu_custom_call" | custom-call | flops 1000000 | bytes 3000000 | tf_op jit(solution)/shard_map/prepare/pallas_call | solution.py:319
  7.2 0.0 collective-permute-done.1
  7.2 0.0 collective-permute-done
  7.3 0.1 maximum_maximum_fusion.image_ref.own_ref
  7.3 4.2 %collective-permute-start.3 = (f32[64,256]{1,0:T(8,128)S(1)}, f32[64,256]{1,0:T(8,128)S(1)}, u32[]{:S(2)}, u32[]{:S(2)}) collective-permute-start(f32[64,256]{1,0:T(8,128)S(1)} %maximum_maximum_fusion.image_ref.own_ref), channel_id=1, source_target_pairs={{4,8},{8,4},{5,9},{9,5},{6,10},{10,6},{7,11},{11,7},{20,24},{24,20... | collective-permute-start | bytes 196616 | tf_op jit(solution)/shard_map/ppermute | solution.py:338
  11.6 0.1 collective-permute-start.2
  11.6 3.5 %own_features.1.kept = bf16[2,2,1248,256]{3,2,1,0:T(8,128)(2,1)S(1)} custom-call(f32[64,256]{1,0:T(8,128)S(1)} %maximum_maximum_fusion.image_ref.own_ref, bf16[512,192]{1,0:T(8,128)(2,1)S(1)} %get-tuple-element.16.t1, bf16[2,256,256]{2,1,0:T(8,128)(2,1)S(1)} %get-tuple-element.17.t2, bf16[2,256,256]{2,1,0:T(8,128)(2,1)S(1)} %get-tuple-element.18.t3, ...), custom_call_target="tpu_custom_call" | custom-call | flops 5000000000 | bytes 10000000 | tf_op jit(solution)/shard_map/own_features/pallas_call | solution.py:339
  15.2 0.0 collective-permute-done.3.odd_ref
  15.2 0.0 collective-permute-done.2.even_ref
  15.2 8.4 %correlate.1 = f32[8,289]{1,0:T(8,128)} custom-call(s32[64,256]{1,0:T(8,128)S(1)} %get-tuple-element.13.choice, f32[8,384]{1,0:T(8,128)S(1)} %get-tuple-element.14.scale, f32[64,256]{1,0:T(8,128)S(1)} %maximum_maximum_fusion.image_ref.own_ref, f32[64,256]{1,0:T(8,128)S(1)} %collective-permute-done.2.even_ref, f32[64,256]{1,0:T(8,128)S(1)} %collective-permute-done.3.odd_ref, ...), custom_call_target="tpu_custom_call" | custom-call | flops 10000000000 | bytes 10000000 | tf_op jit(solution)/shard_map/correlate/pallas_call | solution.py:346
  (2 shorter events, 0.0 us)
Async XLA Ops:
  0.0 7.2 %collective-permute-start.1 = (f32[32,256]{1,0:T(8,128)}, f32[32,256]{1,0:T(8,128)S(1)}, u32[]{:S(2)}, u32[]{:S(2)}) collective-permute-start(f32[32,256]{1,0:T(8,128)} %bitcast.6), channel_id=1, source_target_pairs={{0,1},{1,0},{2,3},{3,2},{4,5},{5,4},{6,7},{7,6},{8,9},{9,8},{10,11... | collective-permute-start | bytes 98312 | tf_op jit(solution)/shard_map/ppermute | solution.py:317
  0.0 7.2 %collective-permute-start = (f32[32,256]{1,0:T(8,128)}, f32[32,256]{1,0:T(8,128)S(1)}, u32[]{:S(2)}, u32[]{:S(2)}) collective-permute-start(f32[32,256]{1,0:T(8,128)} %bitcast.7), channel_id=1, source_target_pairs={{1,2},{2,1},{5,6},{6,5},{9,10},{10,9},{13,14},{14,13},{17,18},{18,... | collective-permute-start | bytes 98312 | tf_op jit(solution)/shard_map/ppermute | solution.py:318
  7.3 7.9 %collective-permute-start.3 = (f32[64,256]{1,0:T(8,128)S(1)}, f32[64,256]{1,0:T(8,128)S(1)}, u32[]{:S(2)}, u32[]{:S(2)}) collective-permute-start(f32[64,256]{1,0:T(8,128)S(1)} %maximum_maximum_fusion.image_ref.own_ref), channel_id=1, source_target_pairs={{4,8},{8,4},{5,9},{9,5},{6,10},{10,6},{7,11},{11,7},{20,24},{24,20... | collective-permute-start | bytes 196616 | tf_op jit(solution)/shard_map/ppermute | solution.py:338
  11.6 3.6 %collective-permute-start.2 = (f32[64,256]{1,0:T(8,128)S(1)}, f32[64,256]{1,0:T(8,128)S(1)}, u32[]{:S(2)}, u32[]{:S(2)}) collective-permute-start(f32[64,256]{1,0:T(8,128)S(1)} %maximum_maximum_fusion.image_ref.own_ref), channel_id=1, source_target_pairs={{0,4},{4,0},{8,12},{12,8},{1,5},{5,1},{9,13},{13,9},{2,6},{6,2},{1... | collective-permute-start | bytes 196616 | tf_op jit(solution)/shard_map/ppermute | solution.py:337
